TPU v7x, 128 devices: a whole 4x4x4 slice. The times are simulated.
128 devices in a mesh: ping: 16 (over x, z), band: 8 (over y, core).
Axes of the slice: x: 4, y: 4, z: 4, core: 2. Of those that a mesh axis runs over, the one named last changes fastest.
Arguments:
- echoes: bfloat16 [2048, 8, 2, 8192], P(('ping', 'band')), may hold values from -6 to 6
- replica: bfloat16 [8, 2, 128], replicated, may hold values from -0.375 to 0.375
- steering: bfloat16 [2, 64, 64], replicated, may hold values from -0.5 to 0.5
- angle_weights: bfloat16 [2, 128, 64], replicated, may hold values from -0.75 to 0.75
- range_weights: bfloat16 [64, 384, 128], P('band'), may hold values from -0.3125 to 0.3125
- range_offsets: int32 [64], P('band'), may hold values from 0 to 5
- merge_owner: int32 [256], replicated, may hold values from -1 to 15, as said below
- merge_slot: int32 [256], replicated, may hold values from 0 to 7
Outputs:
- merged: bfloat16 [128, 2, 128, 8192], P('ping', None, None, 'band')
Inputs may be any that keep to these rules, and one draw needn't show every extreme that they name: `merge_owner`: -1 marks a block that is not kept. Among the 16 blocks of one ping index (aligned blocks of the list) at most 2 name the same owner, and in every draw one owner is named by exactly 2 blocks of every ping index.
All inputs are finite; a program needn't handle non-finite values.
Results may differ from a plain program's by a relative error of at most 0.007.
Values may be sent and summed in bfloat16 or wider, within the bound.
No kernel may reach another device: no remote copies, remote signals or barrier semaphores. Data moves between devices by JAX's collectives and lax.ppermute only.
A program may use at most 128 MiB of HBM per device.

v0:
```python
import jax
import jax.numpy as jnp
from jax import lax
from jax.sharding import PartitionSpec as P

SUB_PINGS = 8


def toeplitz_blocks(replica):
    taps_count = replica.shape[2]
    shifts = jnp.arange(taps_count)
    row_index = jnp.arange(taps_count)[:, None]
    col_index = jnp.arange(taps_count)[None, :]
    lower_sel = ((row_index - col_index)[None] == shifts[:, None, None]).astype(jnp.float32)
    upper_sel = ((row_index - col_index + taps_count)[None] == shifts[:, None, None]).astype(
        jnp.float32
    )
    real_taps = replica[:, 0].astype(jnp.float32)
    imag_taps = replica[:, 1].astype(jnp.float32)
    high = lax.Precision.HIGHEST
    lower_real = jnp.einsum("ck,kmn->cmn", real_taps, lower_sel, precision=high)
    lower_imag = jnp.einsum("ck,kmn->cmn", imag_taps, lower_sel, precision=high)
    upper_real = jnp.einsum("ck,kmn->cmn", real_taps, upper_sel, precision=high)
    upper_imag = jnp.einsum("ck,kmn->cmn", imag_taps, upper_sel, precision=high)
    layers = [
        jnp.concatenate([lower_real, -lower_imag], 2),
        jnp.concatenate([lower_imag, lower_real], 2),
        jnp.concatenate([upper_real, -upper_imag], 2),
        jnp.concatenate([upper_imag, upper_real], 2),
    ]
    return jnp.concatenate(layers, 1).astype(jnp.bfloat16)


def compress(echo_part, toeplitz):
    pings, chans, parts, bins = echo_part.shape
    taps_count = toeplitz.shape[2] // 2
    block_count = bins // taps_count
    shaped = echo_part.reshape(pings, chans, parts, block_count, taps_count)
    weights = toeplitz.reshape(chans, 2, parts, taps_count, 2, taps_count)
    lower = jnp.einsum(
        "pcqbk,cqkon->pcobn", shaped, weights[:, 0], preferred_element_type=jnp.float32
    )
    upper = jnp.einsum(
        "pcqbk,cqkon->pcobn", shaped, weights[:, 1], preferred_element_type=jnp.float32
    )
    moved = jnp.concatenate([upper[:, :, :, 1:], jnp.zeros_like(upper[:, :, :, :1])], axis=3)
    total = lower + moved
    return total.reshape(pings, chans, 2, bins).astype(jnp.bfloat16)


def beamform(tile, steering, sub_pings):
    pings, chans, parts, bins = tile.shape
    blocks = pings // sub_pings
    grouped = tile.reshape(blocks, sub_pings * chans * parts, bins)
    real_steer = steering[0]
    imag_steer = steering[1]
    beam_count = real_steer.shape[0]
    mixer = jnp.concatenate(
        [
            jnp.concatenate([real_steer, -imag_steer], 1),
            jnp.concatenate([imag_steer, real_steer], 1),
        ],
        0,
    )
    mixer = (
        mixer.reshape(2 * beam_count, 2, sub_pings * chans)
        .transpose(0, 2, 1)
        .reshape(2 * beam_count, -1)
    )
    beams = jnp.einsum("yx,bxr->byr", mixer, grouped, preferred_element_type=jnp.float32)
    return beams.reshape(blocks, 2, beam_count, bins).astype(jnp.bfloat16)


def rotate_angles(beam_image, angle_weights, parity):
    matrices = jnp.where(parity[:, None, None] == 1, angle_weights[1], angle_weights[0])
    turned = jnp.einsum("bya,bpar->bpyr", matrices, beam_image, preferred_element_type=jnp.float32)
    return turned.astype(jnp.bfloat16)


def dense_interp(range_weights, range_offsets):
    count = range_weights.shape[0]
    selector = (
        jnp.arange(count)[None, None, :]
        == (range_offsets[:, None] + jnp.arange(3)[None, :])[:, :, None]
    ).astype(jnp.bfloat16)
    pieces = range_weights.reshape(count, 3, 128, 128)
    dense = jnp.einsum("jtb,jtin->bijn", selector, pieces, preferred_element_type=jnp.float32)
    return dense.astype(jnp.bfloat16).reshape(count * 128, count * 128)


def range_interp(turned, dense):
    flat = turned.reshape(-1, turned.shape[3])
    product = jnp.dot(flat, dense, preferred_element_type=jnp.float32)
    return product.astype(jnp.bfloat16).reshape(turned.shape)


def pack_rows(packer, source):
    flat = jnp.dot(packer, source.reshape(source.shape[0], -1), preferred_element_type=jnp.float32)
    return flat.astype(jnp.bfloat16).reshape((packer.shape[0],) + source.shape[1:])


def on_device(
    echoes, replica, steering, angle_weights, range_weights, range_offsets, merge_owner, merge_slot
):
    ping_count = lax.axis_size("ping")
    ping_index = lax.axis_index("ping")
    toeplitz = toeplitz_blocks(replica)
    compressed = compress(echoes, toeplitz)
    band_tile = lax.all_to_all(compressed, "band", split_axis=3, concat_axis=0, tiled=True)
    beam_image = beamform(band_tile, steering, SUB_PINGS)
    blocks_here = beam_image.shape[0]
    capacity = max(2, (blocks_here + ping_count - 1) // ping_count)
    slot_count = blocks_here // 2
    routes = merge_owner.reshape(ping_count, blocks_here)
    slots_all = merge_slot.reshape(ping_count, blocks_here)
    my_routes = lax.dynamic_index_in_dim(routes, ping_index, 0, keepdims=False)
    target_hot = (my_routes[:, None] == jnp.arange(ping_count)[None, :]).astype(jnp.int32)
    rank_send = jnp.sum(jnp.cumsum(target_hot, 0) * target_hot, 1) - 1
    packer = (target_hot.T[:, None, :] == 1) & (
        rank_send[None, None, :] == jnp.arange(capacity)[None, :, None]
    )
    packer = packer.reshape(ping_count * capacity, blocks_here).astype(jnp.bfloat16)
    owned = (routes == ping_index).astype(jnp.int32)
    rank_recv = jnp.cumsum(owned, 1) * owned - 1
    matched = (owned[:, None, :] == 1) & (
        rank_recv[:, None, :] == jnp.arange(capacity)[None, :, None]
    )
    matched_float = matched.astype(jnp.float32)
    slot_hot = (slots_all[:, :, None] == jnp.arange(slot_count)[None, None, :]).astype(jnp.float32)
    combiner = jnp.einsum("scb,sbo->osc", matched_float, slot_hot).reshape(
        slot_count, ping_count * capacity
    )
    combiner = combiner.astype(jnp.bfloat16)
    dense = dense_interp(range_weights, range_offsets)
    my_parity = (ping_index * blocks_here + jnp.arange(blocks_here)) % 2
    images = range_interp(rotate_angles(beam_image, angle_weights, my_parity), dense)
    outgoing = pack_rows(packer, images)
    arrived = lax.all_to_all(outgoing, "ping", split_axis=0, concat_axis=0, tiled=True)
    merged = jnp.dot(
        combiner, arrived.reshape(arrived.shape[0], -1), preferred_element_type=jnp.float32
    )
    return merged.reshape((slot_count,) + arrived.shape[1:]).astype(jnp.bfloat16)


def solution(mesh):
    placed = (
        P(("ping", "band"), None, None, None),
        P(),
        P(),
        P(),
        P("band", None, None),
        P("band"),
        P(),
        P(),
    )
    return jax.shard_map(
        on_device,
        mesh=mesh,
        in_specs=placed,
        out_specs=P("ping", None, None, "band"),
        check_vma=False,
    )
```

profile of v0, /device:TPU:68, one launch (start us, length us, event | category | flops | bytes accessed | tf_op | source)
XLA Modules:
  0.0 673.4 jit_solution(3247890180094275025)
XLA Ops:
  0.0 0.8 fusion.50
  0.8 1.3 fusion.3
  2.2 1.3 fusion.27
  3.5 1.3 fusion.28
  4.8 1.4 fusion.30
  6.3 9.5 %maximum_maximum_fusion = bf16[8,512,256]{2,0,1:T(8,128)(2,1)S(1)} fusion(bf16[8,128,128]{2,0,1:T(8,128)(2,1)S(1)} %fusion.27, bf16[8,128,128]{2,0,1:T(8,128)(2,1)S(1)} %get-tuple-element.21, bf16[8,128,128]{2,0,1:T(8,128)(2,1)S(1)} %get-tuple-element.22, bf16[8,128,128]{2,0,1:T(8,128)(2,1)S(1)} %fusion.28, bf16[8,128,128]{2,0,1:T(8,128)(2,1)S(1)} %get-tuple-element.10, ...), kind=kLoop, calls=%fused_computation.26 | loop fusion | flops 16777216 | bytes 3670016 | tf_op jit(solution)/shard_map/concatenate | solution.py:31
  15.8 0.4 fusion.48
  16.1 7.8 %reshape.188 = bf16[16,8,2,64,128]{4,3,2,1,0:T(8,128)(2,1)} reshape(bf16[16,8,2,8192]{3,2,1,0:T(2,128)(2,1)} %param.8) | data formatting | bytes 8388608 | tf_op jit(solution)/shard_map/reshape | solution.py:38
  24.0 6.7 fusion.15
  30.6 4.7 slice.38
  35.3 2.9 fusion.2
  38.3 48.6 %copy.68 = bf16[16,8,2,64,128]{0,2,1,4,3:T(2,128)(2,1)} copy(bf16[16,8,2,64,128]{4,3,0,2,1:T(8,128)(2,1)} %fusion.2) | data formatting | bytes 8388608 | tf_op jit(solution)/shard_map/convert_element_type | solution.py:48
  86.9 38.1 %reshape.209 = bf16[8,2,131072]{2,1,0:T(2,128)(2,1)} reshape(bf16[8192,8,2,16]{3,2,1,0:T(2,128)(2,1)} %bitcast.128) | data formatting | bytes 8388608
  125.0 4.7 all-to-all-start
  130.2 1.2 convert_bitcast_fusion
  131.4 2.7 copy.49
  134.3 0.2 select_reduce_fusion
  134.6 44.8 %all-to-all-done = bf16[8,2,131072]{2,1,0:T(2,128)(2,1)} async-done(((bf16[8,2,131072]{2,1,0:T(2,128)(2,1)}), bf16[8,2,131072]{2,1,0:T(2,128)(2,1)}, u32[]{:S(2)}, u32[]{:S(2)}) %all-to-all-start) | async-done | bytes 4194336 | tf_op jit(solution)/shard_map/all_to_all | solution.py:109
  179.4 25.7 %reshape.210 = bf16[8192,8,2,16]{3,2,1,0:T(2,128)(2,1)} reshape(bf16[8,2,131072]{2,1,0:T(2,128)(2,1)} %all-to-all-done) | data formatting | bytes 8388608
  205.1 76.8 %copy.43 = bf16[16,8,2,8,1024]{4,2,1,0,3:T(2,128)(2,1)} copy(bf16[16,8,2,8,1024]{0,2,1,4,3:T(2,128)(2,1)} %bitcast.129) | data formatting | bytes 8388608 | tf_op jit(solution)/shard_map/all_to_all | solution.py:109
  281.9 7.2 %reshape.189 = bf16[16,128,1024]{2,1,0:T(8,128)(2,1)} reshape(bf16[8,16,8,2,1024]{4,3,2,1,0:T(2,128)(2,1)} %bitcast.132) | data formatting | bytes 8388608 | tf_op jit(solution)/shard_map/reshape | solution.py:54
  289.1 3.7 convolution_convert_fusion.3
  292.8 2.4 convolution_convert_fusion.2
  295.3 12.4 %convolution_convert_fusion.1 = bf16[4096,1024]{1,0:T(8,128)(2,1)} fusion(bf16[4096,1024]{1,0:T(8,128)(2,1)S(1)} %bitcast.134, bf16[128,8,8,128]{3,2,1,0:T(8,128)(2,1)} %bitcast.136), kind=kOutput, calls=%fused_computation.11 | convolution fusion | flops 8594128896 | bytes 18874368 | tf_op jit(solution)/shard_map/dot_general | solution.py:93
  307.7 8.1 %reshape_reshape.3 = bf16[16,262144]{1,0:T(8,128)(2,1)} reshape(bf16[4096,1024]{1,0:T(8,128)(2,1)} %convolution_convert_fusion.1) | data formatting | bytes 16777216 | tf_op jit(solution)/shard_map/reshape;reshape | solution.py:98
  315.8 13.6 %convolution_convert_fusion = bf16[32,262144]{1,0:T(8,128)(2,1)} fusion(pred[32,16]{1,0:T(32,128)(4,1)S(1)} %and.49, bf16[16,262144]{1,0:T(8,128)(2,1)} %reshape_reshape.3), kind=kOutput, calls=%fused_computation | convolution fusion | flops 276824064 | bytes 25166336 | tf_op jit(solution)/shard_map/dot_general | solution.py:98
  329.4 18.7 %copy.77 = bf16[4,8,256,1024]{3,2,1,0:T(8,128)(2,1)} copy(bf16[4,8,256,1024]{3,1,2,0:T(8,128)(2,1)} %bitcast.131) | data formatting | bytes 33554432
  348.1 7.9 %all-to-all-start.1 = ((bf16[32,2,128,1024]{3,2,1,0:T(8,128)(2,1)}), bf16[32,2,128,1024]{3,2,1,0:T(8,128)(2,1)}, u32[]{:S(2)}, u32[]{:S(2)}) async-start(bf16[32,2,128,1024]{3,2,1,0:T(8,128)(2,1)} %bitcast.130), calls=%async_computation.1 | async-start | bytes 33554432 | tf_op jit(solution)/shard_map/all_to_all | solution.py:138
  356.0 0.2 reduce_window_sum.22
  356.5 295.7 %all-to-all-done.1 = bf16[32,2,128,1024]{3,2,1,0:T(8,128)(2,1)} async-done(((bf16[32,2,128,1024]{3,2,1,0:T(8,128)(2,1)}), bf16[32,2,128,1024]{3,2,1,0:T(8,128)(2,1)}, u32[]{:S(2)}, u32[]{:S(2)}) %all-to-all-start.1) | async-done | bytes 16777248 | tf_op jit(solution)/shard_map/all_to_all | solution.py:138
  652.1 16.6 %fusion.20 = bf16[8,2,128,1024]{3,0,2,1:T(8,128)(2,1)S(1)} fusion(bf16[8,32,1,1]{0,1,3,2:T(8,128)(2,1)S(1)} %bitcast.141, bf16[2,128,1024,32]{2,1,0,3:T(8,128)(2,1)} %bitcast.76), kind=kOutput, calls=%fused_computation.22 | convolution fusion | flops 136314880 | bytes 20972032 | tf_op jit(solution)/shard_map/dot_general | solution.py:139
  668.8 4.4 copy.52
  (40 shorter events, 1.0 us)
Async XLA Ops:
  0.0 130.2 %copy-start = (bf16[8,384,128]{2,1,0:T(8,128)(2,1)S(1)}, bf16[8,384,128]{2,1,0:T(8,128)(2,1)}, u32[]{:S(2)}) copy-start(bf16[8,384,128]{2,1,0:T(8,128)(2,1)} %param.12) | copy-start | bytes 2359300
  30.6 4.7 copy-start.2
  125.0 4.7 copy-start.3
  125.0 5.1 copy-start.7
  125.0 54.4 %all-to-all-start = ((bf16[8,2,131072]{2,1,0:T(2,128)(2,1)}), bf16[8,2,131072]{2,1,0:T(2,128)(2,1)}, u32[]{:S(2)}, u32[]{:S(2)}) async-start(bf16[8,2,131072]{2,1,0:T(2,128)(2,1)} %reshape.209), calls=%async_computation | async-start | bytes 8388608 | tf_op jit(solution)/shard_map/all_to_all | solution.py:109
  129.7 4.4 copy-start.5
  129.7 4.8 copy-start.4
  348.1 8.1 %copy-start.6 = (s32[256]{0:T(256)S(1)}, s32[256]{0:T(256)}, u32[]{:S(2)}) copy-start(s32[256]{0:T(256)} %param.15) | copy-start | bytes 3076
  348.1 304.0 %all-to-all-start.1 = ((bf16[32,2,128,1024]{3,2,1,0:T(8,128)(2,1)}), bf16[32,2,128,1024]{3,2,1,0:T(8,128)(2,1)}, u32[]{:S(2)}, u32[]{:S(2)}) async-start(bf16[32,2,128,1024]{3,2,1,0:T(8,128)(2,1)} %bitcast.130), calls=%async_computation.1 | async-start | bytes 33554432 | tf_op jit(solution)/shard_map/all_to_all | solution.py:138
  652.1 21.0 %copy-start.1 = (bf16[8,384,128]{2,1,0:T(8,128)(2,1)S(1)}, bf16[8,384,128]{2,1,0:T(8,128)(2,1)}, u32[]{:S(2)}) copy-start(bf16[8,384,128]{2,1,0:T(8,128)(2,1)} %param.12) | copy-start | bytes 2359300
where the time goes:
time: 684 us; the launch traced here: 673 us
  waiting for transfers between devices  340 us (50%)
  local copies, waits for them, and re-layouts  244 us (36%)
  matrix products  65.2 us (10%)
  starting transfers between devices  12.6 us (2%)
  other arithmetic  10.2 us (1%)
    all_to_all x1, waiting for transfers between devices, on_device(): lax.all_to_all(outgoing, 'ping', split_axis=0, concat_axis=0, tiled=True)  296 us
    unnamed x21, local copies, waits for them, and re-layouts  82.7 us
    all_to_all x1, local copies, waits for them, and re-layouts, on_device(): lax.all_to_all(compressed, 'band', split_axis=3, concat_axis=0, tiled=True)  76.8 us
    convert_element_type x1, local copies, waits for them, and re-layouts, compress(): return total.reshape(pings, chans, 2, bins).astype(jnp.bfloat16)  48.6 us
    all_to_all x1, waiting for transfers between devices, on_device(): lax.all_to_all(compressed, 'band', split_axis=3, concat_axis=0, tiled=True)  44.8 us
    dot_general x1, matrix products, on_device(): jnp.dot(combiner, arrived.reshape(arrived.shape[0], -1), preferred_elemen...  16.6 us
  transfers between devices with their start and end apart: 2, of which 2 were waited for; matrix products, arithmetic and copies ran while one was open for 1% of the time, Pallas kernels for 0%

commit v1 on v0

v1 whole, which is shorter than its diff:
```python
import functools

import jax
import jax.numpy as jnp
from jax import lax
from jax.experimental import pallas as pl
from jax.experimental.pallas import tpu as pltpu
from jax.sharding import PartitionSpec as P

CHUNKS = 1
VMEM_LIMIT = 56 * 1024 * 1024


def compress_kernel(x_ref, taps_ref, out_ref):
    row = lax.broadcasted_iota(jnp.int32, (128, 128), 0)
    col = lax.broadcasted_iota(jnp.int32, (128, 128), 1)
    lower, upper = [], []
    for part in range(2):
        line = jnp.broadcast_to(taps_ref[0, part : part + 1, :], (128, 128))
        circulant = pltpu.roll(line, 0, 1, stride=1, stride_axis=0)
        lower.append(jnp.where(row >= col, circulant, 0.0))
        upper.append(jnp.where(row < col, circulant, 0.0))
    weights = jnp.concatenate(
        [
            jnp.concatenate([lower[0], -lower[1]], 1),
            jnp.concatenate([lower[1], lower[0]], 1),
            jnp.concatenate([upper[0], -upper[1]], 1),
            jnp.concatenate([upper[1], upper[0]], 1),
        ],
        0,
    ).astype(jnp.bfloat16)
    wanted = (row & 7) * 16 + ((row >> 3) & 7) * 2 + (row >> 6)
    permute = (wanted == col).astype(jnp.float32).astype(jnp.bfloat16)
    for block in range(2):
        real, imag = [], []
        for tile in range(8):
            rows = x_ref[8 * block : 8 * block + 8, 0, 16 * tile : 16 * tile + 16, :]
            moved = jnp.dot(permute, rows.reshape(128, 128), preferred_element_type=jnp.float32)
            real.append(moved[:64])
            imag.append(moved[64:])
        real = jnp.concatenate(real, 0)
        imag = jnp.concatenate(imag, 0)
        nothing = jnp.zeros((8, 128), jnp.float32)
        real_next = jnp.concatenate([real[8:], nothing], 0)
        imag_next = jnp.concatenate([imag[8:], nothing], 0)
        stacked = jnp.concatenate([real, imag, real_next, imag_next], 1).astype(jnp.bfloat16)
        product = jnp.dot(stacked, weights, preferred_element_type=jnp.float32)
        product = product.reshape(64, 8, 256)
        product = jnp.concatenate([product[:, :, :128], product[:, :, 128:]], 1)
        out_ref[:, block, :, 0] = product.astype(jnp.bfloat16).reshape(8, 8, 16, 128)


def compress(x, taps, first, count):
    return pl.pallas_call(
        compress_kernel,
        grid=(count,),
        in_specs=[
            pl.BlockSpec((16, 1, 128, 128), lambda i: (0, first + i, 0, 0)),
            pl.BlockSpec((1, 2, 128), lambda i: (first + i, 0, 0)),
        ],
        out_specs=pl.BlockSpec((8, 2, 8, 1, 16, 128), lambda i: (0, 0, 0, i, 0, 0)),
        out_shape=jax.ShapeDtypeStruct((8, 2, 8, count, 16, 128), jnp.bfloat16),
        compiler_params=pltpu.CompilerParams(vmem_limit_bytes=VMEM_LIMIT),
        name="compress",
    )(x, taps)


def pack_kernel(table_ref, source_ref, out_ref, sems):
    def copy(slot):
        block = jnp.maximum(table_ref[slot], 0)
        return pltpu.make_async_copy(source_ref.at[block], out_ref.at[slot], sems.at[slot])

    for slot in range(32):
        copy(slot).start()
    for slot in range(32):
        copy(slot).wait()


def pack(table, source):
    return pl.pallas_call(
        pack_kernel,
        grid_spec=pltpu.PrefetchScalarGridSpec(
            num_scalar_prefetch=1,
            grid=(1,),
            in_specs=[pl.BlockSpec(memory_space=pl.ANY)],
            out_specs=pl.BlockSpec(memory_space=pl.ANY),
            scratch_shapes=[pltpu.SemaphoreType.DMA((32,))],
        ),
        out_shape=jax.ShapeDtypeStruct((32,) + source.shape[1:], source.dtype),
        name="pack",
    )(table, source)


def image_kernel(chunks, ids_ref, offsets_ref, *refs):
    arrived = refs[:chunks]
    angle_ref, range_ref, out_ref, total, turned = refs[chunks:]
    step = pl.program_id(0)
    height = 128 // chunks

    @pl.when(step < 8)
    def _():
        total[...] = jnp.zeros_like(total)

        def add(slot, carry):
            target = ids_ref[slot]

            @pl.when(target >= 0)
            def _():
                for chunk in range(chunks):
                    rows = pl.ds(chunk * height, height)
                    total[target, rows, :] += arrived[chunk][slot, 0].astype(jnp.float32)

            return carry

        lax.fori_loop(0, 32, add, 0)
        angle = angle_ref[...]
        for image in range(8):
            both = total[2 * image : 2 * image + 2].reshape(256, 128).astype(jnp.bfloat16)
            product = jnp.dot(angle, both, preferred_element_type=jnp.float32)
            turned[step, 256 * image : 256 * image + 256, :] = product.astype(jnp.bfloat16)

    @pl.when(step >= 8)
    def _():
        start = offsets_ref[jnp.maximum(step - 8, 0)]
        for half in range(2):
            rows = pl.ds(1024 * half, 1024)
            slab = jnp.concatenate([turned[start + i, rows, :] for i in range(3)], 1)
            product = jnp.dot(slab, range_ref[0], preferred_element_type=jnp.float32)
            out_ref[rows, :] = product.astype(jnp.bfloat16)


def form_images(ids, offsets, arrived, angle, range_weights):
    chunks = len(arrived)
    height = 128 // chunks
    return pl.pallas_call(
        functools.partial(image_kernel, chunks),
        grid_spec=pltpu.PrefetchScalarGridSpec(
            num_scalar_prefetch=2,
            grid=(16,),
            in_specs=[pl.BlockSpec((32, 1, height, 128), lambda s, *_: (0, jnp.minimum(s, 7), 0, 0))]
            * chunks
            + [
                pl.BlockSpec((256, 256), lambda s, *_: (0, 0)),
                pl.BlockSpec((1, 384, 128), lambda s, *_: (jnp.maximum(s - 8, 0), 0, 0)),
            ],
            out_specs=pl.BlockSpec((2048, 128), lambda s, *_: (0, jnp.maximum(s - 8, 0))),
            scratch_shapes=[
                pltpu.VMEM((16, 128, 128), jnp.float32),
                pltpu.VMEM((8, 2048, 128), jnp.bfloat16),
            ],
        ),
        out_shape=jax.ShapeDtypeStruct((2048, 1024), jnp.bfloat16),
        compiler_params=pltpu.CompilerParams(vmem_limit_bytes=VMEM_LIMIT),
        name="form_images",
    )(ids, offsets, *arrived, angle, range_weights)


def angle_matrix(steering, angle_weights):
    both = jnp.einsum("pya,sae->pyse", angle_weights, steering, preferred_element_type=jnp.float32)
    real, imag = both[:, :, 0], both[:, :, 1]
    full = jnp.stack([jnp.stack([real, -imag], 2), jnp.stack([imag, real], 2)], 0)
    full = full.astype(jnp.bfloat16).reshape(2, 2, 128, 2, 8, 8)
    return full.transpose(0, 2, 1, 5, 3, 4).reshape(256, 256)


def routing(merge_owner, merge_slot, ping_index):
    owners = merge_owner.reshape(16, 16)
    slots = merge_slot.reshape(16, 16)
    place = jnp.arange(16, dtype=jnp.int32)
    same = (owners[:, :, None] == owners[:, None, :]) & (place[None, :, None] > place[None, None, :])
    rank = jnp.sum(same.astype(jnp.int32), 2)
    pair = jnp.arange(2, dtype=jnp.int32)
    mine = lax.dynamic_index_in_dim(owners, ping_index, 0, keepdims=False)
    my_rank = lax.dynamic_index_in_dim(rank, ping_index, 0, keepdims=False)
    leaving = (mine[None, None, :] == place[:, None, None]) & (my_rank[None, None, :] == pair[None, :, None])
    table = jnp.sum(jnp.where(leaving, place[None, None, :] + 1, 0), 2) - 1
    coming = (owners[:, None, :] == ping_index) & (rank[:, None, :] == pair[None, :, None])
    target = slots * 2 + place[None, :] % 2
    ids = jnp.sum(jnp.where(coming, target[:, None, :] + 1, 0), 2) - 1
    return table.reshape(32), ids.reshape(32)


def on_device(echoes, replica, steering, angle_weights, range_weights, range_offsets, merge_owner, merge_slot):
    ping_index = lax.axis_index("ping")
    x = echoes.reshape(16, 8, 2, 64, 128).transpose(0, 1, 3, 2, 4).reshape(16, 8, 128, 128)
    taps = jnp.roll(jnp.flip(replica, 2), 1, 2).astype(jnp.float32)
    table, ids = routing(merge_owner, merge_slot, ping_index)
    angle = angle_matrix(steering, angle_weights)
    width = 8 // CHUNKS
    arrived = []
    for chunk in range(CHUNKS):
        sent = compress(x, taps, width * chunk, width)
        band_tile = lax.all_to_all(sent, "band", split_axis=0, concat_axis=0, tiled=True)
        blocks = band_tile.reshape(16, 8, width * 16, 128)
        outgoing = pack(table, blocks)
        arrived.append(lax.all_to_all(outgoing, "ping", split_axis=0, concat_axis=0, tiled=True))
    merged = form_images(ids, range_offsets, arrived, angle, range_weights)
    return merged.reshape(8, 2, 128, 1024)


def solution(mesh):
    placed = (
        P(("ping", "band"), None, None, None),
        P(),
        P(),
        P(),
        P("band", None, None),
        P("band"),
        P(),
        P(),
    )
    return jax.shard_map(
        on_device,
        mesh=mesh,
        in_specs=placed,
        out_specs=P("ping", None, None, "band"),
        check_vma=False,
    )
```

time: 684 us -> 495 us (0.72)
  the two profiles are of different devices: /device:TPU:68 before, /device:TPU:0 now
where the time goes in v1:
time: 495 us; the launch traced here: 493 us
  Pallas kernels  283 us (57%)
  waiting for transfers between devices  191 us (39%)
  starting transfers between devices  12.7 us (3%)
    pallas_call x1, Pallas kernels, pack(): pl.pallas_call(pack_kernel, grid_spec=pltpu.PrefetchScalarGridSpec(num_sc...  256 us
    all_to_all x1, waiting for transfers between devices, on_device(): lax.all_to_all(outgoing, 'ping', split_axis=0, concat_axis=0, tiled=True)  142 us
    all_to_all x1, waiting for transfers between devices, on_device(): lax.all_to_all(sent, 'band', split_axis=0, concat_axis=0, tiled=True)  48.2 us
    pallas_call x1, Pallas kernels, form_images(): pl.pallas_call(functools.partial(image_kernel, chunks), grid_spec=pltpu.P...  18 us
  transfers between devices with their start and end apart: 2, of which 2 were waited for; matrix products, arithmetic and copies ran while one was open for 1% of the time, Pallas kernels for 0%

profile of v1, /device:TPU:0, one launch (start us, length us, event | category | flops | bytes accessed | tf_op | source)
XLA Modules:
  0.0 492.9 jit_solution(11135186583436544675)
XLA Ops:
  0.0 0.0 copy-start
  0.0 0.8 slice.19
  0.8 0.1 slice.20
  0.9 1.4 maximum_convert_fusion.taps_ref
  2.2 8.9 %compress.1 = bf16[8,2,8,8,16,128]{5,4,3,2,1,0:T(8,128)(2,1)} custom-call(bf16[16,8,128,128]{3,2,1,0:T(8,128)(2,1)} %bitcast.32, f32[8,2,128]{2,1,0:T(2,128)} %maximum_convert_fusion.taps_ref), custom_call_target="tpu_custom_call" | custom-call | tf_op jit(solution)/shard_map/compress/pallas_call | solution.py:54
  11.2 0.0 copy-start.2
  11.2 4.7 all-to-all-start
  15.9 0.0 copy-done.2
  15.9 0.1 broadcast_in_dim_reshape.2
  16.0 0.4 convert_reduce_fusion
  16.5 0.1 select_reduce_fusion
  16.6 0.1 copy.19
  16.7 0.7 sub.13.table_ref
  17.4 48.2 %all-to-all-done = bf16[8,2,8,8,16,128]{5,4,3,2,1,0:T(8,128)(2,1)} async-done(((bf16[8,2,8,8,16,128]{5,4,3,2,1,0:T(8,128)(2,1)}), bf16[8,2,8,8,16,128]{5,4,3,2,1,0:T(8,128)(2,1)}, u32[]{:S(2)}, u32[]{:S(2)}) %all-to-all-start) | async-done | bytes 4194336 | tf_op jit(solution)/shard_map/all_to_all | solution.py:193
  65.6 256.2 %pack.1 = bf16[32,8,128,128]{3,2,1,0:T(8,128)(2,1)} custom-call(s32[32]{0:T(128)} %sub.13.table_ref, bf16[16,8,128,128]{3,2,1,0:T(8,128)(2,1)} %bitcast.5.source_ref), custom_call_target="tpu_custom_call" | custom-call | tf_op jit(solution)/shard_map/pack/pallas_call | solution.py:80
  321.8 0.0 copy-start.3
  321.8 0.0 copy-start.1
  321.8 8.0 %all-to-all-start.1 = ((bf16[32,8,128,128]{3,2,1,0:T(8,128)(2,1)}), bf16[32,8,128,128]{3,2,1,0:T(8,128)(2,1)}, u32[]{:S(2)}, u32[]{:S(2)}) async-start(bf16[32,8,128,128]{3,2,1,0:T(8,128)(2,1)} %pack.1), calls=%async_computation.1 | async-start | bytes 16777216 | tf_op jit(solution)/shard_map/all_to_all | solution.py:196
  329.8 0.0 copy-done.3
  329.8 0.1 mul.15
  329.9 0.1 select_reduce_fusion.1
  330.1 0.1 copy.18
  330.1 0.7 sub.11.ids_ref
  330.8 0.0 copy-done
  330.8 0.0 copy-done.1
  330.8 0.2 fusion
  331.1 0.1 copy.23
  331.2 0.1 copy.22
  331.3 0.3 pad_maximum_fusion
  331.6 0.8 copy.24.refs_1_
  332.4 142.4 %all-to-all-done.1.refs_0_ = bf16[32,8,128,128]{3,2,1,0:T(8,128)(2,1)} async-done(((bf16[32,8,128,128]{3,2,1,0:T(8,128)(2,1)}), bf16[32,8,128,128]{3,2,1,0:T(8,128)(2,1)}, u32[]{:S(2)}, u32[]{:S(2)}) %all-to-all-start.1) | async-done | bytes 8388640 | tf_op jit(solution)/shard_map/all_to_all | solution.py:196
  474.9 18.0 %form_images.1 = bf16[2048,1024]{1,0:T(8,128)(2,1)} custom-call(s32[32]{0:T(128)} %sub.11.ids_ref, s32[8]{0:T(128)} %offsets_ref.1, bf16[32,8,128,128]{3,2,1,0:T(8,128)(2,1)} %all-to-all-done.1.refs_0_, bf16[256,256]{1,0:T(8,128)(2,1)} %copy.24.refs_1_, bf16[8,384,128]{2,1,0:T(8,128)(2,1)} %refs_2_.1), custom_call_target="tpu_custom_call" | custom-call | tf_op jit(solution)/shard_map/form_images/pallas_call | solution.py:135
  (15 shorter events, 0.1 us)
Async XLA Ops:
  0.0 330.8 %copy-start = (bf16[2,128,64]{1,2,0:T(8,128)(2,1)S(1)}, bf16[2,128,64]{1,2,0:T(8,128)(2,1)}, u32[]{:S(2)}) copy-start(bf16[2,128,64]{1,2,0:T(8,128)(2,1)} %param.11) | copy-start | bytes 98308
  11.2 4.8 copy-start.2
  11.2 54.5 %all-to-all-start = ((bf16[8,2,8,8,16,128]{5,4,3,2,1,0:T(8,128)(2,1)}), bf16[8,2,8,8,16,128]{5,4,3,2,1,0:T(8,128)(2,1)}, u32[]{:S(2)}, u32[]{:S(2)}) async-start(bf16[8,2,8,8,16,128]{5,4,3,2,1,0:T(8,128)(2,1)} %compress.1), calls=%async_computation | async-start | bytes 8388608 | tf_op jit(solution)/shard_map/all_to_all | solution.py:193
  321.8 8.0 %copy-start.3 = (s32[256]{0:T(256)S(1)}, s32[256]{0:T(256)}, u32[]{:S(2)}) copy-start(s32[256]{0:T(256)} %param.15) | copy-start | bytes 3076
  321.8 9.0 %copy-start.1 = (bf16[2,64,64]{2,1,0:T(8,128)(2,1)S(1)}, bf16[2,64,64]{2,1,0:T(8,128)(2,1)}, u32[]{:S(2)}) copy-start(bf16[2,64,64]{2,1,0:T(8,128)(2,1)} %param.10) | copy-start | bytes 49156
  321.8 153.0 %all-to-all-start.1 = ((bf16[32,8,128,128]{3,2,1,0:T(8,128)(2,1)}), bf16[32,8,128,128]{3,2,1,0:T(8,128)(2,1)}, u32[]{:S(2)}, u32[]{:S(2)}) async-start(bf16[32,8,128,128]{3,2,1,0:T(8,128)(2,1)} %pack.1), calls=%async_computation.1 | async-start | bytes 16777216 | tf_op jit(solution)/shard_map/all_to_all | solution.py:196

commit v2 on v1

--- a/solution.py
+++ b/solution.py
@@ -65,15 +65,28 @@
     )(x, taps)
 
 
-def pack_kernel(table_ref, source_ref, out_ref, sems):
-    def copy(slot):
-        block = jnp.maximum(table_ref[slot], 0)
-        return pltpu.make_async_copy(source_ref.at[block], out_ref.at[slot], sems.at[slot])
-
-    for slot in range(32):
-        copy(slot).start()
-    for slot in range(32):
-        copy(slot).wait()
+def pack_kernel(table_ref, source_ref, out_ref, held, in_sems, out_sems):
+    def fetch(block):
+        return pltpu.make_async_copy(source_ref.at[block], held.at[block], in_sems.at[block])
+
+    def send(block):
+        slot = jnp.maximum(table_ref[block], 0)
+        return pltpu.make_async_copy(held.at[block], out_ref.at[slot], out_sems.at[block])
+
+    for block in range(16):
+        fetch(block).start()
+    for block in range(16):
+        fetch(block).wait()
+
+        @pl.when(table_ref[block] >= 0)
+        def _():
+            send(block).start()
+
+    for block in range(16):
+
+        @pl.when(table_ref[block] >= 0)
+        def _():
+            send(block).wait()
 
 
 def pack(table, source):
@@ -84,9 +97,14 @@
             grid=(1,),
             in_specs=[pl.BlockSpec(memory_space=pl.ANY)],
             out_specs=pl.BlockSpec(memory_space=pl.ANY),
-            scratch_shapes=[pltpu.SemaphoreType.DMA((32,))],
+            scratch_shapes=[
+                pltpu.VMEM(source.shape, source.dtype),
+                pltpu.SemaphoreType.DMA((16,)),
+                pltpu.SemaphoreType.DMA((16,)),
+            ],
         ),
         out_shape=jax.ShapeDtypeStruct((32,) + source.shape[1:], source.dtype),
+        compiler_params=pltpu.CompilerParams(vmem_limit_bytes=VMEM_LIMIT),
         name="pack",
     )(table, source)
 
@@ -169,15 +187,13 @@
     place = jnp.arange(16, dtype=jnp.int32)
     same = (owners[:, :, None] == owners[:, None, :]) & (place[None, :, None] > place[None, None, :])
     rank = jnp.sum(same.astype(jnp.int32), 2)
+    leaving = jnp.where(owners >= 0, owners * 2 + rank, -1)
+    table = lax.dynamic_index_in_dim(leaving, ping_index, 0, keepdims=False)
     pair = jnp.arange(2, dtype=jnp.int32)
-    mine = lax.dynamic_index_in_dim(owners, ping_index, 0, keepdims=False)
-    my_rank = lax.dynamic_index_in_dim(rank, ping_index, 0, keepdims=False)
-    leaving = (mine[None, None, :] == place[:, None, None]) & (my_rank[None, None, :] == pair[None, :, None])
-    table = jnp.sum(jnp.where(leaving, place[None, None, :] + 1, 0), 2) - 1
     coming = (owners[:, None, :] == ping_index) & (rank[:, None, :] == pair[None, :, None])
     target = slots * 2 + place[None, :] % 2
     ids = jnp.sum(jnp.where(coming, target[:, None, :] + 1, 0), 2) - 1
-    return table.reshape(32), ids.reshape(32)
+    return table, ids.reshape(32)
 
 
 def on_device(echoes, replica, steering, angle_weights, range_weights, range_offsets, merge_owner, merge_slot):

time: 495 us -> 243 us (0.49)
  Pallas kernels: 283 us -> 31.8 us
    pallas_call x1, Pallas kernels: 256 us -> 4.52 us  [pack(): pl.pallas_call(pack_kernel, grid_spec=pltpu.PrefetchScalarGridSpec(num_sc...]
where the time goes in v2:
time: 243 us; the launch traced here: 241 us
  waiting for transfers between devices  191 us (79%)
  Pallas kernels  31.8 us (13%)
  starting transfers between devices  12.6 us (5%)
  other arithmetic  2.81 us (1%)
  local copies, waits for them, and re-layouts  2.8 us (1%)
    all_to_all x1, waiting for transfers between devices, on_device(): lax.all_to_all(outgoing, 'ping', split_axis=0, concat_axis=0, tiled=True)  142 us
    all_to_all x1, waiting for transfers between devices, on_device(): lax.all_to_all(sent, 'band', split_axis=0, concat_axis=0, tiled=True)  48.6 us
    pallas_call x1, Pallas kernels, form_images(): pl.pallas_call(functools.partial(image_kernel, chunks), grid_spec=pltpu.P...  18.4 us
    pallas_call x1, Pallas kernels, compress(): pl.pallas_call(compress_kernel, grid=(count,), in_specs=[pl.BlockSpec((16...  8.94 us
    all_to_all x1, starting transfers between devices, on_device(): lax.all_to_all(outgoing, 'ping', split_axis=0, concat_axis=0, tiled=True)  7.82 us
  transfers between devices with their start and end apart: 2, of which 2 were waited for; matrix products, arithmetic and copies ran while one was open for 1% of the time, Pallas kernels for 0%

profile of v2, /device:TPU:0, one launch (start us, length us, event | category | flops | bytes accessed | tf_op | source)
XLA Modules:
  0.0 241.4 jit_solution(4727145726882981493)
XLA Ops:
  0.0 0.0 copy-start
  0.0 0.8 slice.19
  0.8 0.1 slice.20
  0.9 1.4 maximum_convert_fusion.taps_ref
  2.2 8.9 %compress.1 = bf16[8,2,8,8,16,128]{5,4,3,2,1,0:T(8,128)(2,1)} custom-call(bf16[16,8,128,128]{3,2,1,0:T(8,128)(2,1)} %bitcast.30, f32[8,2,128]{2,1,0:T(2,128)} %maximum_convert_fusion.taps_ref), custom_call_target="tpu_custom_call" | custom-call | tf_op jit(solution)/shard_map/compress/pallas_call | solution.py:54
  11.2 0.0 copy-start.2
  11.2 4.7 %all-to-all-start = ((bf16[8,2,8,8,16,128]{5,4,3,2,1,0:T(8,128)(2,1)}), bf16[8,2,8,8,16,128]{5,4,3,2,1,0:T(8,128)(2,1)}, u32[]{:S(2)}, u32[]{:S(2)}) async-start(bf16[8,2,8,8,16,128]{5,4,3,2,1,0:T(8,128)(2,1)} %compress.1), calls=%async_computation | async-start | bytes 8388608 | tf_op jit(solution)/shard_map/all_to_all | solution.py:209
  15.9 0.0 copy-done.2
  15.9 0.1 broadcast_in_dim_reshape.2
  16.0 0.4 convert_reduce_fusion
  16.5 0.5 fusion.4.table_ref
  17.0 48.6 %all-to-all-done = bf16[8,2,8,8,16,128]{5,4,3,2,1,0:T(8,128)(2,1)} async-done(((bf16[8,2,8,8,16,128]{5,4,3,2,1,0:T(8,128)(2,1)}), bf16[8,2,8,8,16,128]{5,4,3,2,1,0:T(8,128)(2,1)}, u32[]{:S(2)}, u32[]{:S(2)}) %all-to-all-start) | async-done | bytes 4194336 | tf_op jit(solution)/shard_map/all_to_all | solution.py:209
  65.6 4.5 %pack.1 = bf16[32,8,128,128]{3,2,1,0:T(8,128)(2,1)} custom-call(s32[16]{0:T(128)} %fusion.4.table_ref, bf16[16,8,128,128]{3,2,1,0:T(8,128)(2,1)} %bitcast.4.source_ref), custom_call_target="tpu_custom_call" | custom-call | tf_op jit(solution)/shard_map/pack/pallas_call | solution.py:93
  70.2 0.0 copy-start.3
  70.2 0.0 copy-start.1
  70.2 7.8 %all-to-all-start.1 = ((bf16[32,8,128,128]{3,2,1,0:T(8,128)(2,1)}), bf16[32,8,128,128]{3,2,1,0:T(8,128)(2,1)}, u32[]{:S(2)}, u32[]{:S(2)}) async-start(bf16[32,8,128,128]{3,2,1,0:T(8,128)(2,1)} %pack.1), calls=%async_computation.1 | async-start | bytes 16777216 | tf_op jit(solution)/shard_map/all_to_all | solution.py:212
  78.0 0.0 copy-done.3
  78.0 0.1 mul.14
  78.1 0.1 select_reduce_fusion
  78.3 0.1 copy.18
  78.3 0.7 sub.7.ids_ref
  79.0 0.0 copy-done
  79.0 0.0 copy-done.1
  79.0 0.2 fusion
  79.3 0.1 copy.22
  79.4 0.1 copy.21
  79.5 0.3 pad_maximum_fusion
  79.9 0.8 copy.23.refs_1_
  80.6 142.4 %all-to-all-done.1.refs_0_ = bf16[32,8,128,128]{3,2,1,0:T(8,128)(2,1)} async-done(((bf16[32,8,128,128]{3,2,1,0:T(8,128)(2,1)}), bf16[32,8,128,128]{3,2,1,0:T(8,128)(2,1)}, u32[]{:S(2)}, u32[]{:S(2)}) %all-to-all-start.1) | async-done | bytes 8388640 | tf_op jit(solution)/shard_map/all_to_all | solution.py:212
  223.1 18.4 %form_images.1 = bf16[2048,1024]{1,0:T(8,128)(2,1)} custom-call(s32[32]{0:T(128)} %sub.7.ids_ref, s32[8]{0:T(128)} %offsets_ref.1, bf16[32,8,128,128]{3,2,1,0:T(8,128)(2,1)} %all-to-all-done.1.refs_0_, bf16[256,256]{1,0:T(8,128)(2,1)} %copy.23.refs_1_, bf16[8,384,128]{2,1,0:T(8,128)(2,1)} %refs_2_.1), custom_call_target="tpu_custom_call" | custom-call | tf_op jit(solution)/shard_map/form_images/pallas_call | solution.py:153
  (10 shorter events, 0.1 us)
Async XLA Ops:
  0.0 79.0 %copy-start = (bf16[2,128,64]{1,2,0:T(8,128)(2,1)S(1)}, bf16[2,128,64]{1,2,0:T(8,128)(2,1)}, u32[]{:S(2)}) copy-start(bf16[2,128,64]{1,2,0:T(8,128)(2,1)} %param.11) | copy-start | bytes 98308
  11.2 4.8 %copy-start.2 = (s32[256]{0:T(256)S(1)}, s32[256]{0:T(256)}, u32[]{:S(2)}) copy-start(s32[256]{0:T(256)} %param.14) | copy-start | bytes 3076
  11.2 54.5 %all-to-all-start = ((bf16[8,2,8,8,16,128]{5,4,3,2,1,0:T(8,128)(2,1)}), bf16[8,2,8,8,16,128]{5,4,3,2,1,0:T(8,128)(2,1)}, u32[]{:S(2)}, u32[]{:S(2)}) async-start(bf16[8,2,8,8,16,128]{5,4,3,2,1,0:T(8,128)(2,1)} %compress.1), calls=%async_computation | async-start | bytes 8388608 | tf_op jit(solution)/shard_map/all_to_all | solution.py:209
  70.2 7.9 %copy-start.3 = (s32[256]{0:T(256)S(1)}, s32[256]{0:T(256)}, u32[]{:S(2)}) copy-start(s32[256]{0:T(256)} %param.15) | copy-start | bytes 3076
  70.2 8.9 %copy-start.1 = (bf16[2,64,64]{2,1,0:T(8,128)(2,1)S(1)}, bf16[2,64,64]{2,1,0:T(8,128)(2,1)}, u32[]{:S(2)}) copy-start(bf16[2,64,64]{2,1,0:T(8,128)(2,1)} %param.10) | copy-start | bytes 49156
  70.2 152.9 %all-to-all-start.1 = ((bf16[32,8,128,128]{3,2,1,0:T(8,128)(2,1)}), bf16[32,8,128,128]{3,2,1,0:T(8,128)(2,1)}, u32[]{:S(2)}, u32[]{:S(2)}) async-start(bf16[32,8,128,128]{3,2,1,0:T(8,128)(2,1)} %pack.1), calls=%async_computation.1 | async-start | bytes 16777216 | tf_op jit(solution)/shard_map/all_to_all | solution.py:212

commit v3 on v2

--- a/solution.py
+++ b/solution.py
@@ -111,9 +111,13 @@
 
 def image_kernel(chunks, ids_ref, offsets_ref, *refs):
     arrived = refs[:chunks]
-    angle_ref, range_ref, out_ref, total, turned = refs[chunks:]
+    angle_ref, range_ref, out_ref, total, turned, angle = refs[chunks:]
     step = pl.program_id(0)
     height = 128 // chunks
+
+    @pl.when(step == 0)
+    def _():
+        angle[...] = jnp.transpose(angle_ref[...].astype(jnp.float32)).astype(jnp.bfloat16)
 
     @pl.when(step < 8)
     def _():
@@ -131,10 +135,9 @@
             return carry
 
         lax.fori_loop(0, 32, add, 0)
-        angle = angle_ref[...]
         for image in range(8):
             both = total[2 * image : 2 * image + 2].reshape(256, 128).astype(jnp.bfloat16)
-            product = jnp.dot(angle, both, preferred_element_type=jnp.float32)
+            product = jnp.dot(angle[...], both, preferred_element_type=jnp.float32)
             turned[step, 256 * image : 256 * image + 256, :] = product.astype(jnp.bfloat16)
 
     @pl.when(step >= 8)
@@ -165,6 +168,7 @@
             scratch_shapes=[
                 pltpu.VMEM((16, 128, 128), jnp.float32),
                 pltpu.VMEM((8, 2048, 128), jnp.bfloat16),
+                pltpu.VMEM((256, 256), jnp.bfloat16),
             ],
         ),
         out_shape=jax.ShapeDtypeStruct((2048, 1024), jnp.bfloat16),
@@ -178,7 +182,7 @@
     real, imag = both[:, :, 0], both[:, :, 1]
     full = jnp.stack([jnp.stack([real, -imag], 2), jnp.stack([imag, real], 2)], 0)
     full = full.astype(jnp.bfloat16).reshape(2, 2, 128, 2, 8, 8)
-    return full.transpose(0, 2, 1, 5, 3, 4).reshape(256, 256)
+    return full.transpose(1, 5, 3, 4, 0, 2).reshape(256, 256)
 
 
 def routing(merge_owner, merge_slot, ping_index):
@@ -206,6 +210,7 @@
     arrived = []
     for chunk in range(CHUNKS):
         sent = compress(x, taps, width * chunk, width)
+        sent, table, ids, angle = lax.optimization_barrier((sent, table, ids, angle))
         band_tile = lax.all_to_all(sent, "band", split_axis=0, concat_axis=0, tiled=True)
         blocks = band_tile.reshape(16, 8, width * 16, 128)
         outgoing = pack(table, blocks)

time: 243 us -> 199 us (0.82)
  waiting for transfers between devices: 191 us -> 0 us
  blocking collectives: 0 us -> 159 us
  starting transfers between devices: 12.6 us -> 0 us
    all_to_all x2 -> x0, waiting for transfers between devices: 191 us -> none  [the longest x1 142 us: on_device(): lax.all_to_all(outgoing, 'ping', split_axis=0, concat_axis=0, tiled=True)]
    all_to_all x0 -> x2, blocking collectives: none -> 159 us  [the longest x1 104 us: on_device(): lax.all_to_all(outgoing, 'ping', split_axis=0, concat_axis=0, tiled=True)]
    all_to_all x2 -> x0, starting transfers between devices: 12.6 us -> none  [the longest x1 7.82 us: on_device(): lax.all_to_all(outgoing, 'ping', split_axis=0, concat_axis=0, tiled=True)]
  transfers between devices with their start and end apart: 2 -> 0, of which waited for: 2 -> 0; matrix products, arithmetic and copies ran while one was open for 1% -> 0% of each run, Pallas kernels for 0% -> 0%
where the time goes in v3:
time: 199 us; the launch traced here: 198 us
  blocking collectives  159 us (80%)
  Pallas kernels  31.3 us (16%)
  other arithmetic  3.86 us (2%)
  local copies, waits for them, and re-layouts  3.26 us (2%)
    all_to_all x1, blocking collectives, on_device(): lax.all_to_all(outgoing, 'ping', split_axis=0, concat_axis=0, tiled=True)  104 us
    all_to_all x1, blocking collectives, on_device(): lax.all_to_all(sent, 'band', split_axis=0, concat_axis=0, tiled=True)  55 us
    pallas_call x1, Pallas kernels, form_images(): pl.pallas_call(functools.partial(image_kernel, chunks), grid_spec=pltpu.P...  18.1 us
    pallas_call x1, Pallas kernels, compress(): pl.pallas_call(compress_kernel, grid=(count,), in_specs=[pl.BlockSpec((16...  8.93 us
    pallas_call x1, Pallas kernels, pack(): pl.pallas_call(pack_kernel, grid_spec=pltpu.PrefetchScalarGridSpec(num_sc...  4.31 us

profile of v3, /device:TPU:0, one launch (start us, length us, event | category | flops | bytes accessed | tf_op | source)
XLA Modules:
  0.0 198.0 jit_solution(5746461881319152722)
XLA Ops:
  0.0 0.0 copy-start
  0.0 0.7 copy-done
  0.8 1.0 fusion
  1.8 0.7 broadcast_multiply_fusion
  2.4 0.8 slice.19
  3.2 0.1 slice.20
  3.3 0.1 mul.15
  3.4 0.8 reshape.93
  4.2 0.4 convert_reduce_fusion
  4.6 0.6 fusion.4.table_ref
  5.2 0.1 select_reduce_fusion
  5.3 0.1 copy.18
  5.4 0.7 sub.7.ids_ref
  6.1 1.4 maximum_convert_fusion.taps_ref
  7.5 0.7 pad_maximum_fusion
  8.1 8.9 %compress.1 = bf16[8,2,8,8,16,128]{5,4,3,2,1,0:T(8,128)(2,1)} custom-call(bf16[16,8,128,128]{3,2,1,0:T(8,128)(2,1)} %bitcast.26, f32[8,2,128]{2,1,0:T(2,128)} %maximum_convert_fusion.taps_ref), custom_call_target="tpu_custom_call" | custom-call | tf_op jit(solution)/shard_map/compress/pallas_call | solution.py:54
  17.1 55.0 %all_to_all.10 = bf16[8,2,8,8,16,128]{5,4,3,2,1,0:T(8,128)(2,1)} all-to-all(bf16[8,2,8,8,16,128]{5,4,3,2,1,0:T(8,128)(2,1)} %compress.1), channel_id=1, replica_groups=mesh['ping'=16,'band'=8] {'band'}, dimensions={0} | all-to-all | bytes 8388608 | tf_op jit(solution)/shard_map/all_to_all | solution.py:214
  72.1 4.3 %pack.1 = bf16[32,8,128,128]{3,2,1,0:T(8,128)(2,1)} custom-call(s32[16]{0:T(128)} %fusion.4.table_ref, bf16[16,8,128,128]{3,2,1,0:T(8,128)(2,1)} %bitcast.25), custom_call_target="tpu_custom_call" | custom-call | tf_op jit(solution)/shard_map/pack/pallas_call | solution.py:93
  76.4 103.6 %all_to_all.11.refs_0_ = bf16[32,8,128,128]{3,2,1,0:T(8,128)(2,1)} all-to-all(bf16[32,8,128,128]{3,2,1,0:T(8,128)(2,1)} %pack.1), channel_id=1, replica_groups=mesh['ping'=16,'band'=8] {'ping'}, dimensions={0} | all-to-all | bytes 16777216 | tf_op jit(solution)/shard_map/all_to_all | solution.py:217
  180.0 18.1 %form_images.1 = bf16[2048,1024]{1,0:T(8,128)(2,1)} custom-call(s32[32]{0:T(128)} %sub.7.ids_ref, s32[8]{0:T(128)} %offsets_ref.1, bf16[32,8,128,128]{3,2,1,0:T(8,128)(2,1)} %all_to_all.11.refs_0_, bf16[256,256]{1,0:T(8,128)(2,1)} %bitcast.27, bf16[8,384,128]{2,1,0:T(8,128)(2,1)} %refs_2_.1), custom_call_target="tpu_custom_call" | custom-call | tf_op jit(solution)/shard_map/form_images/pallas_call | solution.py:156
  (10 shorter events, 0.1 us)
Async XLA Ops:
  0.0 0.8 copy-start

commit v4 on v3

--- a/solution.py
+++ b/solution.py
@@ -7,11 +7,11 @@
 from jax.experimental.pallas import tpu as pltpu
 from jax.sharding import PartitionSpec as P
 
-CHUNKS = 1
+SPLIT = 4
 VMEM_LIMIT = 56 * 1024 * 1024
 
 
-def compress_kernel(x_ref, taps_ref, out_ref):
+def compress_kernel(relative, band_ref, x_ref, taps_ref, *refs):
     row = lax.broadcasted_iota(jnp.int32, (128, 128), 0)
     col = lax.broadcasted_iota(jnp.int32, (128, 128), 1)
     lower, upper = [], []
@@ -47,30 +47,60 @@
         product = jnp.dot(stacked, weights, preferred_element_type=jnp.float32)
         product = product.reshape(64, 8, 256)
         product = jnp.concatenate([product[:, :, :128], product[:, :, 128:]], 1)
-        out_ref[:, block, :, 0] = product.astype(jnp.bfloat16).reshape(8, 8, 16, 128)
-
-
-def compress(x, taps, first, count):
+        product = product.astype(jnp.bfloat16).reshape(8, 8, 16, 128)
+        if not relative:
+            refs[0][:, block, :, 0] = product
+            continue
+        held = refs[4]
+        held[...] = product
+        for step in range(4):
+            for other in range(2):
+                refs[step][other, block, :, 0] = held[band_at(band_ref[0], step, other)]
+
+
+def band_at(band, step, other):
+    return ((band >> 1) + step) % 4 * 2 + ((band & 1) + other) % 2
+
+
+def compress(band, x, taps, first, count, relative):
+    lead, outs = (2, 4) if relative else (8, 1)
     return pl.pallas_call(
-        compress_kernel,
-        grid=(count,),
-        in_specs=[
-            pl.BlockSpec((16, 1, 128, 128), lambda i: (0, first + i, 0, 0)),
-            pl.BlockSpec((1, 2, 128), lambda i: (first + i, 0, 0)),
-        ],
-        out_specs=pl.BlockSpec((8, 2, 8, 1, 16, 128), lambda i: (0, 0, 0, i, 0, 0)),
-        out_shape=jax.ShapeDtypeStruct((8, 2, 8, count, 16, 128), jnp.bfloat16),
+        functools.partial(compress_kernel, relative),
+        grid_spec=pltpu.PrefetchScalarGridSpec(
+            num_scalar_prefetch=1,
+            grid=(count,),
+            in_specs=[
+                pl.BlockSpec((16, 1, 128, 128), lambda i, *_: (0, first + i, 0, 0)),
+                pl.BlockSpec((1, 2, 128), lambda i, *_: (first + i, 0, 0)),
+            ],
+            out_specs=[pl.BlockSpec((lead, 2, 8, 1, 16, 128), lambda i, *_: (0, 0, 0, i, 0, 0))] * outs,
+            scratch_shapes=[pltpu.VMEM((8, 8, 16, 128), jnp.bfloat16)] * relative,
+        ),
+        out_shape=[jax.ShapeDtypeStruct((lead, 2, 8, count, 16, 128), jnp.bfloat16)] * outs,
         compiler_params=pltpu.CompilerParams(vmem_limit_bytes=VMEM_LIMIT),
-        name="compress",
-    )(x, taps)
-
-
-def pack_kernel(table_ref, source_ref, out_ref, held, in_sems, out_sems):
+        name="compress_relative" if relative else "compress",
+    )(band, x, taps)
+
+
+def pack_kernel(relative, table_ref, band_ref, *refs):
+    sources, (out_ref, held, in_sems, out_sems) = refs[:-4], refs[-4:]
+
+    def source(block):
+        if not relative:
+            return sources[0].at[block // 2, block % 2]
+        step, other = block // 4, block // 2 % 2
+        return sources[4].at[step, block % 2] if other else sources[step].at[0, block % 2]
+
+    def name(block):
+        if not relative:
+            return block
+        return 2 * band_at(band_ref[0], 4 - block // 4, block // 2 % 2) + block % 2
+
     def fetch(block):
-        return pltpu.make_async_copy(source_ref.at[block], held.at[block], in_sems.at[block])
+        return pltpu.make_async_copy(source(block), held.at[block], in_sems.at[block])
 
     def send(block):
-        slot = jnp.maximum(table_ref[block], 0)
+        slot = jnp.maximum(table_ref[name(block)], 0)
         return pltpu.make_async_copy(held.at[block], out_ref.at[slot], out_sems.at[block])
 
     for block in range(16):
@@ -78,42 +108,43 @@
     for block in range(16):
         fetch(block).wait()
 
-        @pl.when(table_ref[block] >= 0)
+        @pl.when(table_ref[name(block)] >= 0)
         def _():
             send(block).start()
 
     for block in range(16):
 
-        @pl.when(table_ref[block] >= 0)
+        @pl.when(table_ref[name(block)] >= 0)
         def _():
             send(block).wait()
 
 
-def pack(table, source):
+def pack(table, band, *sources):
+    shape, kind = sources[0].shape[2:], sources[0].dtype
     return pl.pallas_call(
-        pack_kernel,
+        functools.partial(pack_kernel, len(sources) > 1),
         grid_spec=pltpu.PrefetchScalarGridSpec(
-            num_scalar_prefetch=1,
+            num_scalar_prefetch=2,
             grid=(1,),
-            in_specs=[pl.BlockSpec(memory_space=pl.ANY)],
+            in_specs=[pl.BlockSpec(memory_space=pl.ANY)] * len(sources),
             out_specs=pl.BlockSpec(memory_space=pl.ANY),
             scratch_shapes=[
-                pltpu.VMEM(source.shape, source.dtype),
+                pltpu.VMEM((16,) + shape, kind),
                 pltpu.SemaphoreType.DMA((16,)),
                 pltpu.SemaphoreType.DMA((16,)),
             ],
         ),
-        out_shape=jax.ShapeDtypeStruct((32,) + source.shape[1:], source.dtype),
+        out_shape=jax.ShapeDtypeStruct((32,) + shape, kind),
         compiler_params=pltpu.CompilerParams(vmem_limit_bytes=VMEM_LIMIT),
         name="pack",
-    )(table, source)
+    )(table, band, *sources)
 
 
 def image_kernel(chunks, ids_ref, offsets_ref, *refs):
     arrived = refs[:chunks]
     angle_ref, range_ref, out_ref, total, turned, angle = refs[chunks:]
     step = pl.program_id(0)
-    height = 128 // chunks
+    heights = [part.shape[2] for part in arrived]
 
     @pl.when(step == 0)
     def _():
@@ -129,7 +160,7 @@
             @pl.when(target >= 0)
             def _():
                 for chunk in range(chunks):
-                    rows = pl.ds(chunk * height, height)
+                    rows = pl.ds(sum(heights[:chunk]), heights[chunk])
                     total[target, rows, :] += arrived[chunk][slot, 0].astype(jnp.float32)
 
             return carry
@@ -152,14 +183,15 @@
 
 def form_images(ids, offsets, arrived, angle, range_weights):
     chunks = len(arrived)
-    height = 128 // chunks
     return pl.pallas_call(
         functools.partial(image_kernel, chunks),
         grid_spec=pltpu.PrefetchScalarGridSpec(
             num_scalar_prefetch=2,
             grid=(16,),
-            in_specs=[pl.BlockSpec((32, 1, height, 128), lambda s, *_: (0, jnp.minimum(s, 7), 0, 0))]
-            * chunks
+            in_specs=[
+                pl.BlockSpec((32, 1, part.shape[2], 128), lambda s, *_: (0, jnp.minimum(s, 7), 0, 0))
+                for part in arrived
+            ]
             + [
                 pl.BlockSpec((256, 256), lambda s, *_: (0, 0)),
                 pl.BlockSpec((1, 384, 128), lambda s, *_: (jnp.maximum(s - 8, 0), 0, 0)),
@@ -200,21 +232,43 @@
     return table, ids.reshape(32)
 
 
+def to_owners(some, outgoing):
+    def exchange(blocks):
+        return lax.all_to_all(blocks, "ping", split_axis=0, concat_axis=0, tiled=True)
+
+    return lax.cond(some, exchange, lambda blocks: blocks, outgoing)
+
+
+def flat(part):
+    return part.reshape(part.shape[:3] + (-1, 128))
+
+
+def ring_step(step, other):
+    return [(band, ((band // 2 + step) % 4) * 2 + (band + other) % 2) for band in range(8)]
+
+
 def on_device(echoes, replica, steering, angle_weights, range_weights, range_offsets, merge_owner, merge_slot):
     ping_index = lax.axis_index("ping")
     x = echoes.reshape(16, 8, 2, 64, 128).transpose(0, 1, 3, 2, 4).reshape(16, 8, 128, 128)
     taps = jnp.roll(jnp.flip(replica, 2), 1, 2).astype(jnp.float32)
     table, ids = routing(merge_owner, merge_slot, ping_index)
     angle = angle_matrix(steering, angle_weights)
-    width = 8 // CHUNKS
-    arrived = []
-    for chunk in range(CHUNKS):
-        sent = compress(x, taps, width * chunk, width)
-        sent, table, ids, angle = lax.optimization_barrier((sent, table, ids, angle))
-        band_tile = lax.all_to_all(sent, "band", split_axis=0, concat_axis=0, tiled=True)
-        blocks = band_tile.reshape(16, 8, width * 16, 128)
-        outgoing = pack(table, blocks)
-        arrived.append(lax.all_to_all(outgoing, "ping", split_axis=0, concat_axis=0, tiled=True))
+    band_index = lax.axis_index("band")
+    band = band_index.reshape(1).astype(jnp.int32)
+    (sent,) = compress(band, x, taps, 0, SPLIT, False)
+    sent, x, table, ids, angle = lax.optimization_barrier((sent, x, table, ids, angle))
+    band_tile = lax.all_to_all(sent, "band", split_axis=0, concat_axis=0, tiled=True)
+    band_tile, x = lax.optimization_barrier((band_tile, x))
+    ring = compress(band, x, taps, SPLIT, 8 - SPLIT, True)
+    outgoing = pack(table, band, flat(band_tile))
+    outgoing, *ring = lax.optimization_barrier((outgoing, *ring))
+    moved = [ring[0]] + [lax.ppermute(ring[step], "band", ring_step(step, 0)) for step in (1, 2, 3)]
+    first = to_owners(jnp.any(merge_owner >= 0), outgoing)
+    first, *moved = lax.optimization_barrier((first, *moved))
+    others = lax.ppermute(jnp.stack([part[1] for part in moved]), "band", ring_step(0, 1))
+    outgoing = pack(table, band, *[flat(part) for part in moved], flat(others))
+    second = lax.all_to_all(outgoing, "ping", split_axis=0, concat_axis=0, tiled=True)
+    arrived = [first, second]
     merged = form_images(ids, range_offsets, arrived, angle, range_weights)
     return merged.reshape(8, 2, 128, 1024)
 

time: 199 us -> 201 us (1.010)
  blocking collectives: 159 us -> 146 us
  starting transfers between devices: 0 us -> 3.49 us
  Pallas kernels: 31.3 us -> 34.6 us
  local copies, waits for them, and re-layouts: 3.26 us -> 6.44 us
  waiting for transfers between devices: 0 us -> 2.65 us
    all_to_all x0 -> x1, blocking collectives: none -> 57.6 us  [exchange(): lax.all_to_all(blocks, 'ping', split_axis=0, concat_axis=0, tiled=True)]
    all_to_all x1, blocking collectives: 104 us -> 56.2 us  [on_device(): lax.all_to_all(outgoing, 'ping', split_axis=0, concat_axis=0, tiled=True)]
    all_to_all x1, blocking collectives: 55 us -> 32.2 us  [on_device(): lax.all_to_all(sent, 'band', split_axis=0, concat_axis=0, tiled=True)]
    pallas_call x2 -> x4, Pallas kernels: 13.2 us -> 16.9 us  [the longest x2 10.3 us: compress(): pl.pallas_call(functools.partial(compress_kernel, relative), grid_spec=pl...]
    ppermute x0 -> x4, starting transfers between devices: none -> 3.49 us  [the longest x3 3.41 us: on_device(): lax.ppermute(ring[step], 'band', ring_step(step, 0))]
    ppermute x0 -> x4, waiting for transfers between devices: none -> 2.65 us  [the longest x1 2.65 us: on_device(): lax.ppermute(jnp.stack([part[1] for part in moved]), 'band', ring_step(0,...]
    cond x0 -> x2, local copies, waits for them, and re-layouts: none -> 2.24 us
  transfers between devices with their start and end apart: 0 -> 4, of which waited for: 0 -> 1; matrix products, arithmetic and copies ran while one was open for 0% -> 0% of each run, Pallas kernels for 0% -> 0%
where the time goes in v4:
time: 201 us; the launch traced here: 200 us
  blocking collectives  146 us (73%)
  Pallas kernels  34.6 us (17%)
  local copies, waits for them, and re-layouts  6.44 us (3%)
  other arithmetic  4.7 us (2%)
  starting transfers between devices  3.49 us (2%)
  waiting for transfers between devices  2.65 us (1%)
    all_to_all x1, blocking collectives, exchange(): lax.all_to_all(blocks, 'ping', split_axis=0, concat_axis=0, tiled=True)  57.6 us
    all_to_all x1, blocking collectives, on_device(): lax.all_to_all(outgoing, 'ping', split_axis=0, concat_axis=0, tiled=True)  56.2 us
    all_to_all x1, blocking collectives, on_device(): lax.all_to_all(sent, 'band', split_axis=0, concat_axis=0, tiled=True)  32.2 us
    pallas_call x1, Pallas kernels, form_images(): pl.pallas_call(functools.partial(image_kernel, chunks), grid_spec=pltpu.P...  17.7 us
    pallas_call x2, Pallas kernels, compress(): pl.pallas_call(functools.partial(compress_kernel, relative), grid_spec=pl...  10.3 us
    pallas_call x2, Pallas kernels, pack(): pl.pallas_call(functools.partial(pack_kernel, len(sources) > 1), grid_spe...  6.59 us
  transfers between devices with their start and end apart: 4, of which 1 were waited for; matrix products, arithmetic and copies ran while one was open for 0% of the time, Pallas kernels for 0%

profile of v4, /device:TPU:0, one launch (start us, length us, event | category | flops | bytes accessed | tf_op | source)
XLA Modules:
  0.0 199.7 jit_solution(1763318308434507989)
XLA Ops:
  0.0 0.7 copy-done
  0.8 1.0 fusion
  1.8 0.7 broadcast_multiply_fusion
  2.5 0.8 slice.31
  3.2 0.1 slice.32
  3.3 0.1 mul.15
  3.4 0.8 reshape.112
  4.2 0.4 convert_reduce_fusion
  4.6 0.6 fusion.4.table_ref
  5.2 0.1 select_reduce_fusion
  5.3 0.1 copy.18
  5.4 0.6 sub.7.ids_ref
  6.0 1.4 maximum_convert_fusion.taps_ref
  7.4 0.7 pad_maximum_fusion.1
  8.1 5.1 %compress.1 = bf16[8,2,8,4,16,128]{5,4,3,2,1,0:T(8,128)(2,1)} custom-call(s32[1]{0:T(128)} %bitcast.band_ref, bf16[16,8,128,128]{3,2,1,0:T(8,128)(2,1)} %bitcast.31, f32[8,2,128]{2,1,0:T(2,128)} %maximum_convert_fusion.taps_ref), custom_call_target="tpu_custom_call" | custom-call | tf_op jit(solution)/shard_map/compress/pallas_call | solution.py:67
  13.2 32.2 %all_to_all.15 = bf16[8,2,8,4,16,128]{5,4,3,2,1,0:T(8,128)(2,1)} all-to-all(bf16[8,2,8,4,16,128]{5,4,3,2,1,0:T(8,128)(2,1)} %compress.1), channel_id=1, replica_groups=mesh['ping'=16,'band'=8] {'band'}, dimensions={0} | all-to-all | bytes 4194304 | tf_op jit(solution)/shard_map/all_to_all | solution.py:260
  45.3 5.3 %compress_relative.1 = (bf16[2,2,8,4,16,128]{5,4,3,2,1,0:T(8,128)(2,1)}, bf16[2,2,8,4,16,128]{5,4,3,2,1,0:T(8,128)(2,1)}, bf16[2,2,8,4,16,128]{5,4,3,2,1,0:T(8,128)(2,1)}, bf16[2,2,8,4,16,128]{5,4,3,2,1,0:T(8,128)(2,1)}) custom-call(s32[1]{0:T(128)} %bitcast.band_ref, bf16[16,8,128,128]{3,2,1,0:T(8,128)(2,1)} %bitcast.32, ...), custom_call_target="tpu_custom_call" | custom-call | tf_op jit(solution)/shard_map/compress_relative/pallas_call | solution.py:67
  50.6 3.4 %pack.2 = bf16[32,8,64,128]{3,2,1,0:T(8,128)(2,1)} custom-call(s32[16]{0:T(128)} %fusion.4.table_ref, s32[1]{0:T(128)} %bitcast.band_ref, bf16[8,2,8,64,128]{4,3,2,1,0:T(8,128)(2,1)} %bitcast.33), custom_call_target="tpu_custom_call" | custom-call | tf_op jit(solution)/shard_map/pack/pallas_call | solution.py:124
  54.0 0.6 collective-permute-start
  54.6 2.0 %collective-permute-start.1 = (bf16[2,2,8,4,16,128]{5,4,3,2,1,0:T(8,128)(2,1)S(1)}, bf16[2,2,8,4,16,128]{5,4,3,2,1,0:T(8,128)(2,1)S(1)}, u32[]{:S(2)}, u32[]{:S(2)}) collective-permute-start(bf16[2,2,8,4,16,128]{5,4,3,2,1,0:T(8,128)(2,1)S(1)} %copy-done.10), channel_id=1, source_target_pairs={{0,4},{1,5},{2,6},{3,7},{4,0},{5,1},{6,2},{7,3},{8,12},{9,13},{10,... | collective-permute-start | bytes 1572872 | tf_op jit(solution)/shard_map/ppermute | solution.py:265
  56.6 0.8 collective-permute-start.2
  57.4 0.7 compare_reduce_fusion
  58.7 59.9 %conditional.1 = (bf16[32,8,64,128]{3,2,1,0:T(8,128)(2,1)}) conditional(s32[]{:T(128)} %convert_element_type.13, bf16[32,8,64,128]{3,2,1,0:T(8,128)(2,1)} %pack.2, bf16[32,8,64,128]{3,2,1,0:T(8,128)(2,1)} %pack.2), branch_computations={%region_3.4_spmd, %region_4.5_spmd} | conditional | bytes 25165860 | solution.py:239
  58.7 2.2 %copy-done.2 = bf16[32,8,64,128]{3,2,1,0:T(8,128)(2,1)S(1)} copy-done((bf16[32,8,64,128]{3,2,1,0:T(8,128)(2,1)S(1)}, bf16[32,8,64,128]{3,2,1,0:T(8,128)(2,1)}, u32[]{:S(2)}) %copy-start.2) | copy-done | bytes 4194328 | tf_op jit(solution)/shard_map/cond
  61.0 57.6 %all_to_all.14 = bf16[32,8,64,128]{3,2,1,0:T(8,128)(2,1)} all-to-all(bf16[32,8,64,128]{3,2,1,0:T(8,128)(2,1)S(1)} %copy-done.2), channel_id=1, replica_groups=mesh['ping'=16,'band'=8] {'ping'}, dimensions={0} | all-to-all | bytes 8388608 | tf_op jit(solution)/shard_map/cond/branch_1_fun/all_to_all | solution.py:237
  118.7 0.1 pad_maximum_fusion
  118.9 0.1 collective-permute-start.3
  119.0 2.6 %collective-permute-done.3 = bf16[4,2,8,4,16,128]{5,4,3,2,1,0:T(8,128)(2,1)S(1)} collective-permute-done((bf16[4,2,8,4,16,128]{5,4,3,2,1,0:T(8,128)(2,1)S(1)}, bf16[4,2,8,4,16,128]{5,4,3,2,1,0:T(8,128)(2,1)S(1)}, u32[]{:S(2)}, u32[]{:S(2)}) %collective-permute-start.3) | collective-permute-done | bytes 1048608 | tf_op jit(solution)/shard_map/ppermute | solution.py:268
  121.6 0.9 copy-done.7
  122.6 3.2 %pack.3 = bf16[32,8,64,128]{3,2,1,0:T(8,128)(2,1)} custom-call(s32[16]{0:T(128)} %fusion.4.table_ref, s32[1]{0:T(128)} %bitcast.band_ref, bf16[2,2,8,64,128]{4,3,2,1,0:T(8,128)(2,1)} %bitcast.34, bf16[2,2,8,64,128]{4,3,2,1,0:T(8,128)(2,1)} %bitcast.35, bf16[2,2,8,64,128]{4,3,2,1,0:T(8,128)(2,1)} %bitcast.36, bf16[2,2,8,64,128]{4,3,2,1,0:T(8,128)(2,1)} %bitcast.37, ...), custom_call_target="tpu_custom_call" | custom-call | tf_op jit(solution)/shard_map/pack/pallas_call | solution.py:124
  125.8 56.2 %all_to_all.16.refs_1_ = bf16[32,8,64,128]{3,2,1,0:T(8,128)(2,1)} all-to-all(bf16[32,8,64,128]{3,2,1,0:T(8,128)(2,1)} %pack.3), channel_id=1, replica_groups=mesh['ping'=16,'band'=8] {'ping'}, dimensions={0} | all-to-all | bytes 8388608 | tf_op jit(solution)/shard_map/all_to_all | solution.py:270
  182.0 17.7 %form_images.1 = bf16[2048,1024]{1,0:T(8,128)(2,1)} custom-call(s32[32]{0:T(128)} %sub.7.ids_ref, s32[8]{0:T(128)} %offsets_ref.1, bf16[32,8,64,128]{3,2,1,0:T(8,128)(2,1)S(1)} %copy-done.1, bf16[32,8,64,128]{3,2,1,0:T(8,128)(2,1)} %all_to_all.16.refs_1_, bf16[256,256]{1,0:T(8,128)(2,1)} %bitcast.39, bf16[8,384,128]{2,1,0:T(8,128)(2,1)} %refs_3_.1), custom_call_target="tpu_custom_call" | custom-call | tf_op jit(solution)/shard_map/form_images/pallas_call | solution.py:186
  (36 shorter events, 0.2 us)
Async XLA Ops:
  0.0 0.8 copy-start
  50.6 4.0 %copy-start.10 = (bf16[2,2,8,4,16,128]{5,4,3,2,1,0:T(8,128)(2,1)S(1)}, bf16[2,2,8,4,16,128]{5,4,3,2,1,0:T(8,128)(2,1)}, u32[]{:S(2)}) copy-start(bf16[2,2,8,4,16,128]{5,4,3,2,1,0:T(8,128)(2,1)} %get-tuple-element.44) | copy-start | bytes 1572868
  50.6 6.0 %copy-start.9 = (bf16[2,2,8,4,16,128]{5,4,3,2,1,0:T(8,128)(2,1)S(1)}, bf16[2,2,8,4,16,128]{5,4,3,2,1,0:T(8,128)(2,1)}, u32[]{:S(2)}) copy-start(bf16[2,2,8,4,16,128]{5,4,3,2,1,0:T(8,128)(2,1)} %get-tuple-element.45) | copy-start | bytes 1572868
  50.6 6.8 %copy-start.8 = (s32[256]{0:T(256)S(1)}, s32[256]{0:T(256)}, u32[]{:S(2)}) copy-start(s32[256]{0:T(256)} %param.16) | copy-start | bytes 3076
  54.0 64.6 %collective-permute-start = (bf16[2,2,8,4,16,128]{5,4,3,2,1,0:T(8,128)(2,1)}, bf16[2,2,8,4,16,128]{5,4,3,2,1,0:T(8,128)(2,1)S(1)}, u32[]{:S(2)}, u32[]{:S(2)}) collective-permute-start(bf16[2,2,8,4,16,128]{5,4,3,2,1,0:T(8,128)(2,1)} %get-tuple-element.43), channel_id=1, source_target_pairs={{0,2},{1,3},{2,4},{3,5},{4,6},{5,7},{6,0},{7,1},{8,10},{9,11},{10,... | collective-permute-start | bytes 1572872 | tf_op jit(solution)/shard_map/ppermute | solution.py:265
  54.6 64.0 %collective-permute-start.1 = (bf16[2,2,8,4,16,128]{5,4,3,2,1,0:T(8,128)(2,1)S(1)}, bf16[2,2,8,4,16,128]{5,4,3,2,1,0:T(8,128)(2,1)S(1)}, u32[]{:S(2)}, u32[]{:S(2)}) collective-permute-start(bf16[2,2,8,4,16,128]{5,4,3,2,1,0:T(8,128)(2,1)S(1)} %copy-done.10), channel_id=1, source_target_pairs={{0,4},{1,5},{2,6},{3,7},{4,0},{5,1},{6,2},{7,3},{8,12},{9,13},{10,... | collective-permute-start | bytes 1572872 | tf_op jit(solution)/shard_map/ppermute | solution.py:265
  56.6 62.0 %collective-permute-start.2 = (bf16[2,2,8,4,16,128]{5,4,3,2,1,0:T(8,128)(2,1)S(1)}, bf16[2,2,8,4,16,128]{5,4,3,2,1,0:T(8,128)(2,1)S(1)}, u32[]{:S(2)}, u32[]{:S(2)}) collective-permute-start(bf16[2,2,8,4,16,128]{5,4,3,2,1,0:T(8,128)(2,1)S(1)} %copy-done.9), channel_id=1, source_target_pairs={{0,6},{1,7},{2,0},{3,1},{4,2},{5,3},{6,4},{7,5},{8,14},{9,15},{10,... | collective-permute-start | bytes 1572872 | tf_op jit(solution)/shard_map/ppermute | solution.py:265
  58.7 59.9 %copy-start.3 = (bf16[2,2,8,4,16,128]{5,4,3,2,1,0:T(8,128)(2,1)S(1)}, bf16[2,2,8,4,16,128]{5,4,3,2,1,0:T(8,128)(2,1)}, u32[]{:S(2)}) copy-start(bf16[2,2,8,4,16,128]{5,4,3,2,1,0:T(8,128)(2,1)} %get-tuple-element.47) | copy-start | bytes 1572868
  58.7 2.2 %copy-start.2 = (bf16[32,8,64,128]{3,2,1,0:T(8,128)(2,1)S(1)}, bf16[32,8,64,128]{3,2,1,0:T(8,128)(2,1)}, u32[]{:S(2)}) copy-start(bf16[32,8,64,128]{3,2,1,0:T(8,128)(2,1)} %param.1) | copy-start | bytes 12582916 | tf_op jit(solution)/shard_map/cond
  118.6 3.0 %copy-start.4 = (bf16[2,2,8,4,16,128]{5,4,3,2,1,0:T(8,128)(2,1)}, bf16[2,2,8,4,16,128]{5,4,3,2,1,0:T(8,128)(2,1)S(1)}, u32[]{:S(2)}) copy-start(bf16[2,2,8,4,16,128]{5,4,3,2,1,0:T(8,128)(2,1)S(1)} %collective-permute-done) | copy-start | bytes 1572868
  118.6 3.0 %copy-start.5 = (bf16[2,2,8,4,16,128]{5,4,3,2,1,0:T(8,128)(2,1)}, bf16[2,2,8,4,16,128]{5,4,3,2,1,0:T(8,128)(2,1)S(1)}, u32[]{:S(2)}) copy-start(bf16[2,2,8,4,16,128]{5,4,3,2,1,0:T(8,128)(2,1)S(1)} %collective-permute-done.1) | copy-start | bytes 1572868
  118.6 3.0 %copy-start.6 = (bf16[2,2,8,4,16,128]{5,4,3,2,1,0:T(8,128)(2,1)}, bf16[2,2,8,4,16,128]{5,4,3,2,1,0:T(8,128)(2,1)S(1)}, u32[]{:S(2)}) copy-start(bf16[2,2,8,4,16,128]{5,4,3,2,1,0:T(8,128)(2,1)S(1)} %collective-permute-done.2) | copy-start | bytes 1572868
  118.9 2.7 %collective-permute-start.3 = (bf16[4,2,8,4,16,128]{5,4,3,2,1,0:T(8,128)(2,1)S(1)}, bf16[4,2,8,4,16,128]{5,4,3,2,1,0:T(8,128)(2,1)S(1)}, u32[]{:S(2)}, u32[]{:S(2)}) collective-permute-start(bf16[4,2,8,4,16,128]{5,4,3,2,1,0:T(8,128)(2,1)S(1)} %pad_maximum_fusion), channel_id=1, source_target_pairs={{0,1},{1,0},{2,3},{3,2},{4,5},{5,4},{6,7},{7,6},{8,9},{9,8},{10,11... | collective-permute-start | bytes 3145736 | tf_op jit(solution)/shard_map/ppermute | solution.py:268
  121.6 1.0 copy-start.7
  125.8 56.2 %copy-start.1 = (bf16[32,8,64,128]{3,2,1,0:T(8,128)(2,1)S(1)}, bf16[32,8,64,128]{3,2,1,0:T(8,128)(2,1)}, u32[]{:S(2)}) copy-start(bf16[32,8,64,128]{3,2,1,0:T(8,128)(2,1)} %get-tuple-element.56.refs_0_) | copy-start | bytes 12582916

commit v5 on v4

--- a/solution.py
+++ b/solution.py
@@ -7,7 +7,7 @@
 from jax.experimental.pallas import tpu as pltpu
 from jax.sharding import PartitionSpec as P
 
-SPLIT = 4
+SPLIT = 3
 VMEM_LIMIT = 56 * 1024 * 1024
 
 
@@ -16,8 +16,8 @@
     col = lax.broadcasted_iota(jnp.int32, (128, 128), 1)
     lower, upper = [], []
     for part in range(2):
-        line = jnp.broadcast_to(taps_ref[0, part : part + 1, :], (128, 128))
-        circulant = pltpu.roll(line, 0, 1, stride=1, stride_axis=0)
+        line = jnp.broadcast_to(taps_ref[0, part : part + 1, :].astype(jnp.float32), (128, 128))
+        circulant = jnp.transpose(pltpu.roll(line, 0, 1, stride=1, stride_axis=0))
         lower.append(jnp.where(row >= col, circulant, 0.0))
         upper.append(jnp.where(row < col, circulant, 0.0))
     weights = jnp.concatenate(
@@ -150,30 +150,29 @@
     def _():
         angle[...] = jnp.transpose(angle_ref[...].astype(jnp.float32)).astype(jnp.bfloat16)
 
-    @pl.when(step < 8)
+    @pl.when(step < 4)
     def _():
         total[...] = jnp.zeros_like(total)
-
-        def add(slot, carry):
+        for slot in range(32):
             target = ids_ref[slot]
 
             @pl.when(target >= 0)
             def _():
                 for chunk in range(chunks):
                     rows = pl.ds(sum(heights[:chunk]), heights[chunk])
-                    total[target, rows, :] += arrived[chunk][slot, 0].astype(jnp.float32)
-
-            return carry
-
-        lax.fori_loop(0, 32, add, 0)
+                    total[target, :, rows, :] += arrived[chunk][slot].astype(jnp.float32)
+
         for image in range(8):
-            both = total[2 * image : 2 * image + 2].reshape(256, 128).astype(jnp.bfloat16)
-            product = jnp.dot(angle[...], both, preferred_element_type=jnp.float32)
-            turned[step, 256 * image : 256 * image + 256, :] = product.astype(jnp.bfloat16)
-
-    @pl.when(step >= 8)
+            both = [total[2 * image : 2 * image + 2, b].reshape(256, 128) for b in range(2)]
+            both = jnp.concatenate(both, 1).astype(jnp.bfloat16)
+            product = jnp.dot(angle[...], both, preferred_element_type=jnp.float32).astype(jnp.bfloat16)
+            for b in range(2):
+                rows = pl.ds(256 * image, 256)
+                turned[2 * step + b, rows, :] = product[:, 128 * b : 128 * b + 128]
+
+    @pl.when(step >= 4)
     def _():
-        start = offsets_ref[jnp.maximum(step - 8, 0)]
+        start = offsets_ref[jnp.maximum(step - 4, 0)]
         for half in range(2):
             rows = pl.ds(1024 * half, 1024)
             slab = jnp.concatenate([turned[start + i, rows, :] for i in range(3)], 1)
@@ -187,18 +186,18 @@
         functools.partial(image_kernel, chunks),
         grid_spec=pltpu.PrefetchScalarGridSpec(
             num_scalar_prefetch=2,
-            grid=(16,),
+            grid=(12,),
             in_specs=[
-                pl.BlockSpec((32, 1, part.shape[2], 128), lambda s, *_: (0, jnp.minimum(s, 7), 0, 0))
+                pl.BlockSpec((32, 2, part.shape[2], 128), lambda s, *_: (0, jnp.minimum(s, 3), 0, 0))
                 for part in arrived
             ]
             + [
                 pl.BlockSpec((256, 256), lambda s, *_: (0, 0)),
-                pl.BlockSpec((1, 384, 128), lambda s, *_: (jnp.maximum(s - 8, 0), 0, 0)),
-            ],
-            out_specs=pl.BlockSpec((2048, 128), lambda s, *_: (0, jnp.maximum(s - 8, 0))),
+                pl.BlockSpec((1, 384, 128), lambda s, *_: (jnp.maximum(s - 4, 0), 0, 0)),
+            ],
+            out_specs=pl.BlockSpec((2048, 128), lambda s, *_: (0, jnp.maximum(s - 4, 0))),
             scratch_shapes=[
-                pltpu.VMEM((16, 128, 128), jnp.float32),
+                pltpu.VMEM((16, 2, 128, 128), jnp.float32),
                 pltpu.VMEM((8, 2048, 128), jnp.bfloat16),
                 pltpu.VMEM((256, 256), jnp.bfloat16),
             ],
@@ -250,20 +249,18 @@
 def on_device(echoes, replica, steering, angle_weights, range_weights, range_offsets, merge_owner, merge_slot):
     ping_index = lax.axis_index("ping")
     x = echoes.reshape(16, 8, 2, 64, 128).transpose(0, 1, 3, 2, 4).reshape(16, 8, 128, 128)
-    taps = jnp.roll(jnp.flip(replica, 2), 1, 2).astype(jnp.float32)
     table, ids = routing(merge_owner, merge_slot, ping_index)
     angle = angle_matrix(steering, angle_weights)
     band_index = lax.axis_index("band")
     band = band_index.reshape(1).astype(jnp.int32)
-    (sent,) = compress(band, x, taps, 0, SPLIT, False)
-    sent, x, table, ids, angle = lax.optimization_barrier((sent, x, table, ids, angle))
+    (sent,) = compress(band, x, replica, 0, SPLIT, False)
     band_tile = lax.all_to_all(sent, "band", split_axis=0, concat_axis=0, tiled=True)
-    band_tile, x = lax.optimization_barrier((band_tile, x))
-    ring = compress(band, x, taps, SPLIT, 8 - SPLIT, True)
+    ring = compress(band, x, replica, SPLIT, 8 - SPLIT, True)
     outgoing = pack(table, band, flat(band_tile))
-    outgoing, *ring = lax.optimization_barrier((outgoing, *ring))
+    some = jnp.any(merge_owner >= 0)
+    outgoing, ids, angle, some, *ring = lax.optimization_barrier((outgoing, ids, angle, some, *ring))
     moved = [ring[0]] + [lax.ppermute(ring[step], "band", ring_step(step, 0)) for step in (1, 2, 3)]
-    first = to_owners(jnp.any(merge_owner >= 0), outgoing)
+    first = to_owners(some, outgoing)
     first, *moved = lax.optimization_barrier((first, *moved))
     others = lax.ppermute(jnp.stack([part[1] for part in moved]), "band", ring_step(0, 1))
     outgoing = pack(table, band, *[flat(part) for part in moved], flat(others))

time: 201 us -> 181 us (0.900)
  blocking collectives: 146 us -> 114 us
  waiting for transfers between devices: 2.65 us -> 14.2 us
  starting transfers between devices: 3.49 us -> 8.17 us
  Pallas kernels: 34.6 us -> 32 us
    all_to_all x1 -> x0, blocking collectives: 32.2 us -> none  [on_device(): lax.all_to_all(sent, 'band', split_axis=0, concat_axis=0, tiled=True)]
    all_to_all x0 -> x1, waiting for transfers between devices: none -> 11.1 us  [on_device(): lax.all_to_all(sent, 'band', split_axis=0, concat_axis=0, tiled=True)]
    all_to_all x1, blocking collectives: 56.2 us -> 67.2 us  [on_device(): lax.all_to_all(outgoing, 'ping', split_axis=0, concat_axis=0, tiled=True)]
    all_to_all x1, blocking collectives: 57.6 us -> 46.8 us  [exchange(): lax.all_to_all(blocks, 'ping', split_axis=0, concat_axis=0, tiled=True)]
    all_to_all x0 -> x1, starting transfers between devices: none -> 4.69 us  [on_device(): lax.all_to_all(sent, 'band', split_axis=0, concat_axis=0, tiled=True)]
    slice x4, local copies, waits for them, and re-layouts: 0.08 us -> 3.99 us  [on_device(): part[1]]
    pallas_call x1, Pallas kernels: 17.7 us -> 13.8 us  [form_images(): pl.pallas_call(functools.partial(image_kernel, chunks), grid_spec=pltpu.P...]
  transfers between devices with their start and end apart: 4 -> 5, of which waited for: 1 -> 2; matrix products, arithmetic and copies ran while one was open for 0% -> 2% of each run, Pallas kernels for 0% -> 4%
where the time goes in v5:
time: 181 us; the launch traced here: 180 us
  blocking collectives  114 us (63%)
  Pallas kernels  32 us (18%)
  waiting for transfers between devices  14.2 us (8%)
  starting transfers between devices  8.17 us (5%)
  local copies, waits for them, and re-layouts  7.66 us (4%)
  other arithmetic  2.71 us (1%)
    all_to_all x1, blocking collectives, on_device(): lax.all_to_all(outgoing, 'ping', split_axis=0, concat_axis=0, tiled=True)  67.2 us
    all_to_all x1, blocking collectives, exchange(): lax.all_to_all(blocks, 'ping', split_axis=0, concat_axis=0, tiled=True)  46.8 us
    pallas_call x1, Pallas kernels, form_images(): pl.pallas_call(functools.partial(image_kernel, chunks), grid_spec=pltpu.P...  13.8 us
    pallas_call x2, Pallas kernels, compress(): pl.pallas_call(functools.partial(compress_kernel, relative), grid_spec=pl...  11.2 us
    all_to_all x1, waiting for transfers between devices, on_device(): lax.all_to_all(sent, 'band', split_axis=0, concat_axis=0, tiled=True)  11.1 us
    pallas_call x2, Pallas kernels, pack(): pl.pallas_call(functools.partial(pack_kernel, len(sources) > 1), grid_spe...  7.11 us
    all_to_all x1, starting transfers between devices, on_device(): lax.all_to_all(sent, 'band', split_axis=0, concat_axis=0, tiled=True)  4.69 us
    slice x4, local copies, waits for them, and re-layouts, on_device(): part[1]  3.99 us
  transfers between devices with their start and end apart: 5, of which 2 were waited for; matrix products, arithmetic and copies ran while one was open for 2% of the time, Pallas kernels for 4%

profile of v5, /device:TPU:0, one launch (start us, length us, event | category | flops | bytes accessed | tf_op | source)
XLA Modules:
  0.0 179.7 jit_solution(8089183413411037410)
XLA Ops:
  0.0 4.4 %compress.1 = bf16[8,2,8,3,16,128]{5,4,3,2,1,0:T(8,128)(2,1)} custom-call(s32[1]{0:T(128)} %bitcast.1.band_ref, bf16[16,8,128,128]{3,2,1,0:T(8,128)(2,1)} %bitcast.30, bf16[8,2,128]{2,1,0:T(2,128)(2,1)} %taps_ref.3), custom_call_target="tpu_custom_call" | custom-call | tf_op jit(solution)/shard_map/compress/pallas_call | solution.py:67
  4.5 4.7 %all-to-all-start.1 = ((bf16[8,2,8,3,16,128]{5,4,3,2,1,0:T(8,128)(2,1)}), bf16[8,2,8,3,16,128]{5,4,3,2,1,0:T(8,128)(2,1)S(1)}, u32[]{:S(2)}, u32[]{:S(2)}) async-start(bf16[8,2,8,3,16,128]{5,4,3,2,1,0:T(8,128)(2,1)} %compress.1), calls=%async_computation.1 | async-start | bytes 3145728 | tf_op jit(solution)/shard_map/all_to_all | solution.py:257
  9.2 0.1 mul.15
  9.4 0.4 convert_reduce_fusion
  9.8 0.1 select_reduce_fusion
  9.9 6.7 %compress_relative.1 = (bf16[2,2,8,5,16,128]{5,4,3,2,1,0:T(8,128)(2,1)}, bf16[2,2,8,5,16,128]{5,4,3,2,1,0:T(8,128)(2,1)}, bf16[2,2,8,5,16,128]{5,4,3,2,1,0:T(8,128)(2,1)}, bf16[2,2,8,5,16,128]{5,4,3,2,1,0:T(8,128)(2,1)}) custom-call(s32[1]{0:T(128)} %bitcast.1.band_ref, bf16[16,8,128,128]{3,2,1,0:T(8,128)(2,1)} %bitcast.31, bf16[8,2,128]{2,1,0:T(2,128)(2,1)} %taps_ref.3), custom_call_target="tpu_custom_call" | custom-call | tf_op jit(solution)/shard_map/compress_relative/pallas_call | solution.py:67
  16.6 0.1 copy.18
  16.7 0.6 sub.7.ids_ref
  17.4 0.2 fusion
  17.7 0.6 fusion.4.table_ref
  18.3 0.7 compare_reduce_fusion
  18.9 0.7 pad_maximum_fusion.1
  19.6 11.1 %all-to-all-done.1 = bf16[8,2,8,3,16,128]{5,4,3,2,1,0:T(8,128)(2,1)S(1)} async-done(((bf16[8,2,8,3,16,128]{5,4,3,2,1,0:T(8,128)(2,1)}), bf16[8,2,8,3,16,128]{5,4,3,2,1,0:T(8,128)(2,1)S(1)}, u32[]{:S(2)}, u32[]{:S(2)}) %all-to-all-start.1) | async-done | bytes 1572896 | tf_op jit(solution)/shard_map/all_to_all | solution.py:257
  30.7 1.1 copy-done.1
  31.9 3.7 %pack.2 = bf16[32,8,48,128]{3,2,1,0:T(8,128)(2,1)S(1)} custom-call(s32[16]{0:T(128)} %fusion.4.table_ref, s32[1]{0:T(128)} %bitcast.1.band_ref, bf16[8,2,8,48,128]{4,3,2,1,0:T(8,128)(2,1)} %bitcast.32), custom_call_target="tpu_custom_call" | custom-call | tf_op jit(solution)/shard_map/pack/pallas_call | solution.py:124
  35.5 0.6 collective-permute-start
  36.2 2.1 %collective-permute-start.1 = (bf16[2,2,8,5,16,128]{5,4,3,2,1,0:T(8,128)(2,1)}, bf16[2,2,8,5,16,128]{5,4,3,2,1,0:T(8,128)(2,1)}, u32[]{:S(2)}, u32[]{:S(2)}) collective-permute-start(bf16[2,2,8,5,16,128]{5,4,3,2,1,0:T(8,128)(2,1)} %get-tuple-element.36), channel_id=1, source_target_pairs={{0,4},{1,5},{2,6},{3,7},{4,0},{5,1},{6,2},{7,3},{8,12},{9,13},{10,... | collective-permute-start | bytes 1966088 | tf_op jit(solution)/shard_map/ppermute | solution.py:262
  38.2 0.7 collective-permute-start.2
  39.6 47.3 %conditional.1 = (bf16[32,8,48,128]{3,2,1,0:T(8,128)(2,1)S(1)}) conditional(s32[]{:T(128)} %convert_element_type.9, bf16[32,8,48,128]{3,2,1,0:T(8,128)(2,1)S(1)} %pack.2, bf16[32,8,48,128]{3,2,1,0:T(8,128)(2,1)S(1)} %pack.2), branch_computations={%region_3.4_spmd, %region_4.5_spmd} | conditional | bytes 12582920 | solution.py:238
  39.6 0.5 copy.27
  40.2 46.8 %all_to_all.14 = bf16[32,8,48,128]{3,2,1,0:T(8,128)(2,1)S(1)} all-to-all(bf16[32,8,48,128]{3,2,1,0:T(8,128)(2,1)S(1)} %copy.27), channel_id=1, replica_groups=mesh['ping'=16,'band'=8] {'ping'}, dimensions={0} | all-to-all | bytes 6291456 | tf_op jit(solution)/shard_map/cond/branch_1_fun/all_to_all | solution.py:236
  86.9 1.0 slice.20
  87.9 1.0 slice.21
  88.9 1.0 slice.22
  89.9 1.0 slice.23
  90.9 0.2 pad_maximum_fusion
  91.1 0.1 collective-permute-start.3
  91.2 3.0 %collective-permute-done.3 = bf16[4,2,8,5,16,128]{5,4,3,2,1,0:T(8,128)(2,1)S(1)} collective-permute-done((bf16[4,2,8,5,16,128]{5,4,3,2,1,0:T(8,128)(2,1)S(1)}, bf16[4,2,8,5,16,128]{5,4,3,2,1,0:T(8,128)(2,1)S(1)}, u32[]{:S(2)}, u32[]{:S(2)}) %collective-permute-start.3) | collective-permute-done | bytes 1310752 | tf_op jit(solution)/shard_map/ppermute | solution.py:265
  94.2 1.1 copy-done.2
  95.3 3.4 %pack.3 = bf16[32,8,80,128]{3,2,1,0:T(8,128)(2,1)} custom-call(s32[16]{0:T(128)} %fusion.4.table_ref, s32[1]{0:T(128)} %bitcast.1.band_ref, bf16[2,2,8,80,128]{4,3,2,1,0:T(8,128)(2,1)} %bitcast.33, bf16[2,2,8,80,128]{4,3,2,1,0:T(8,128)(2,1)} %bitcast.16.refs_1_, bf16[2,2,8,80,128]{4,3,2,1,0:T(8,128)(2,1)} %bitcast.17.refs_2_, ...), custom_call_target="tpu_custom_call" | custom-call | tf_op jit(solution)/shard_map/pack/pallas_call | solution.py:124
  98.7 67.2 %all_to_all.15.refs_1_ = bf16[32,8,80,128]{3,2,1,0:T(8,128)(2,1)} all-to-all(bf16[32,8,80,128]{3,2,1,0:T(8,128)(2,1)} %pack.3), channel_id=1, replica_groups=mesh['ping'=16,'band'=8] {'ping'}, dimensions={0} | all-to-all | bytes 10485760 | tf_op jit(solution)/shard_map/all_to_all | solution.py:267
  166.0 13.8 %form_images.1 = bf16[2048,1024]{1,0:T(8,128)(2,1)} custom-call(s32[32]{0:T(128)} %sub.7.ids_ref, s32[8]{0:T(128)} %offsets_ref.1, bf16[32,8,48,128]{3,2,1,0:T(8,128)(2,1)S(1)} %get-tuple-element.48.refs_0_, bf16[32,8,80,128]{3,2,1,0:T(8,128)(2,1)} %all_to_all.15.refs_1_, bf16[256,256]{1,0:T(8,128)(2,1)} %bitcast.35, bf16[8,384,128]{2,1,0:T(8,128)(2,1)} %refs_3_.1), custom_call_target="tpu_custom_call" | custom-call | tf_op jit(solution)/shard_map/form_images/pallas_call | solution.py:185
  (25 shorter events, 0.2 us)
Async XLA Ops:
  0.0 17.4 %copy-start = (bf16[2,128,64]{1,2,0:T(8,128)(2,1)S(1)}, bf16[2,128,64]{1,2,0:T(8,128)(2,1)}, u32[]{:S(2)}) copy-start(bf16[2,128,64]{1,2,0:T(8,128)(2,1)} %param.13) | copy-start | bytes 98308
  4.5 4.7 %copy-start.5 = (s32[256]{0:T(256)S(1)}, s32[256]{0:T(256)}, u32[]{:S(2)}) copy-start(s32[256]{0:T(256)} %param.17) | copy-start | bytes 3076
  4.5 4.8 %copy-start.4 = (s32[256]{0:T(256)S(1)}, s32[256]{0:T(256)}, u32[]{:S(2)}) copy-start(s32[256]{0:T(256)} %param.16) | copy-start | bytes 3076
  4.5 26.3 %all-to-all-start.1 = ((bf16[8,2,8,3,16,128]{5,4,3,2,1,0:T(8,128)(2,1)}), bf16[8,2,8,3,16,128]{5,4,3,2,1,0:T(8,128)(2,1)S(1)}, u32[]{:S(2)}, u32[]{:S(2)}) async-start(bf16[8,2,8,3,16,128]{5,4,3,2,1,0:T(8,128)(2,1)} %compress.1), calls=%async_computation.1 | async-start | bytes 3145728 | tf_op jit(solution)/shard_map/all_to_all | solution.py:257
  9.9 7.4 %copy-start.3 = (bf16[2,64,64]{2,1,0:T(8,128)(2,1)S(1)}, bf16[2,64,64]{2,1,0:T(8,128)(2,1)}, u32[]{:S(2)}) copy-start(bf16[2,64,64]{2,1,0:T(8,128)(2,1)} %param.12) | copy-start | bytes 49156
  30.7 1.1 copy-start.1
  35.5 51.4 %collective-permute-start = (bf16[2,2,8,5,16,128]{5,4,3,2,1,0:T(8,128)(2,1)}, bf16[2,2,8,5,16,128]{5,4,3,2,1,0:T(8,128)(2,1)}, u32[]{:S(2)}, u32[]{:S(2)}) collective-permute-start(bf16[2,2,8,5,16,128]{5,4,3,2,1,0:T(8,128)(2,1)} %get-tuple-element.35), channel_id=1, source_target_pairs={{0,2},{1,3},{2,4},{3,5},{4,6},{5,7},{6,0},{7,1},{8,10},{9,11},{10,... | collective-permute-start | bytes 1966088 | tf_op jit(solution)/shard_map/ppermute | solution.py:262
  36.2 50.7 %collective-permute-start.1 = (bf16[2,2,8,5,16,128]{5,4,3,2,1,0:T(8,128)(2,1)}, bf16[2,2,8,5,16,128]{5,4,3,2,1,0:T(8,128)(2,1)}, u32[]{:S(2)}, u32[]{:S(2)}) collective-permute-start(bf16[2,2,8,5,16,128]{5,4,3,2,1,0:T(8,128)(2,1)} %get-tuple-element.36), channel_id=1, source_target_pairs={{0,4},{1,5},{2,6},{3,7},{4,0},{5,1},{6,2},{7,3},{8,12},{9,13},{10,... | collective-permute-start | bytes 1966088 | tf_op jit(solution)/shard_map/ppermute | solution.py:262
  38.2 48.7 %collective-permute-start.2 = (bf16[2,2,8,5,16,128]{5,4,3,2,1,0:T(8,128)(2,1)}, bf16[2,2,8,5,16,128]{5,4,3,2,1,0:T(8,128)(2,1)}, u32[]{:S(2)}, u32[]{:S(2)}) collective-permute-start(bf16[2,2,8,5,16,128]{5,4,3,2,1,0:T(8,128)(2,1)} %get-tuple-element.37), channel_id=1, source_target_pairs={{0,6},{1,7},{2,0},{3,1},{4,2},{5,3},{6,4},{7,5},{8,14},{9,15},{10,... | collective-permute-start | bytes 1966088 | tf_op jit(solution)/shard_map/ppermute | solution.py:262
  91.1 3.1 %collective-permute-start.3 = (bf16[4,2,8,5,16,128]{5,4,3,2,1,0:T(8,128)(2,1)S(1)}, bf16[4,2,8,5,16,128]{5,4,3,2,1,0:T(8,128)(2,1)S(1)}, u32[]{:S(2)}, u32[]{:S(2)}) collective-permute-start(bf16[4,2,8,5,16,128]{5,4,3,2,1,0:T(8,128)(2,1)S(1)} %pad_maximum_fusion), channel_id=1, source_target_pairs={{0,1},{1,0},{2,3},{3,2},{4,5},{5,4},{6,7},{7,6},{8,9},{9,8},{10,11... | collective-permute-start | bytes 3932168 | tf_op jit(solution)/shard_map/ppermute | solution.py:265
  94.2 1.1 copy-start.2

commit v6 on v5

--- a/solution.py
+++ b/solution.py
@@ -51,11 +51,11 @@
         if not relative:
             refs[0][:, block, :, 0] = product
             continue
-        held = refs[4]
+        held = refs[2]
         held[...] = product
         for step in range(4):
             for other in range(2):
-                refs[step][other, block, :, 0] = held[band_at(band_ref[0], step, other)]
+                refs[other][step, block, :, 0] = held[band_at(band_ref[0], step, other)]
 
 
 def band_at(band, step, other):
@@ -63,7 +63,7 @@
 
 
 def compress(band, x, taps, first, count, relative):
-    lead, outs = (2, 4) if relative else (8, 1)
+    lead, outs = (4, 2) if relative else (8, 1)
     return pl.pallas_call(
         functools.partial(compress_kernel, relative),
         grid_spec=pltpu.PrefetchScalarGridSpec(
@@ -89,7 +89,7 @@
         if not relative:
             return sources[0].at[block // 2, block % 2]
         step, other = block // 4, block // 2 % 2
-        return sources[4].at[step, block % 2] if other else sources[step].at[0, block % 2]
+        return sources[step + 1].at[other, block % 2] if step else sources[other].at[0, block % 2]
 
     def name(block):
         if not relative:
@@ -255,15 +255,18 @@
     band = band_index.reshape(1).astype(jnp.int32)
     (sent,) = compress(band, x, replica, 0, SPLIT, False)
     band_tile = lax.all_to_all(sent, "band", split_axis=0, concat_axis=0, tiled=True)
-    ring = compress(band, x, replica, SPLIT, 8 - SPLIT, True)
+    same, other = compress(band, x, replica, SPLIT, 8 - SPLIT, True)
+    other = lax.ppermute(other, "band", ring_step(0, 1))
+    ring = [jnp.stack([same[step], other[step]]) for step in (1, 2, 3)]
     outgoing = pack(table, band, flat(band_tile))
     some = jnp.any(merge_owner >= 0)
-    outgoing, ids, angle, some, *ring = lax.optimization_barrier((outgoing, ids, angle, some, *ring))
-    moved = [ring[0]] + [lax.ppermute(ring[step], "band", ring_step(step, 0)) for step in (1, 2, 3)]
+    outgoing, ids, angle, some, same, other, *ring = lax.optimization_barrier(
+        (outgoing, ids, angle, some, same, other, *ring)
+    )
+    ring = [lax.ppermute(part, "band", ring_step(step + 1, 0)) for step, part in enumerate(ring)]
     first = to_owners(some, outgoing)
-    first, *moved = lax.optimization_barrier((first, *moved))
-    others = lax.ppermute(jnp.stack([part[1] for part in moved]), "band", ring_step(0, 1))
-    outgoing = pack(table, band, *[flat(part) for part in moved], flat(others))
+    first, *ring = lax.optimization_barrier((first, *ring))
+    outgoing = pack(table, band, *[flat(part) for part in (same, other, *ring)])
     second = lax.all_to_all(outgoing, "ping", split_axis=0, concat_axis=0, tiled=True)
     arrived = [first, second]
     merged = form_images(ids, range_offsets, arrived, angle, range_weights)

time: 181 us -> 170 us (0.939)
  waiting for transfers between devices: 14.2 us -> 6.72 us
  local copies, waits for them, and re-layouts: 7.66 us -> 4.16 us
  blocking collectives: 114 us -> 111 us
  other arithmetic: 2.71 us -> 4.9 us
    all_to_all x1, waiting for transfers between devices: 11.1 us -> 6.7 us  [on_device(): lax.all_to_all(sent, 'band', split_axis=0, concat_axis=0, tiled=True)]
    ppermute x4, waiting for transfers between devices: 3.03 us -> 0.01 us  [the longest x3 0.01 us: on_device(): lax.ppermute(part, 'band', ring_step(step + 1, 0))]
    all_to_all x1, blocking collectives: 67.2 us -> 64.3 us  [on_device(): lax.all_to_all(outgoing, 'ping', split_axis=0, concat_axis=0, tiled=True)]
    slice x4 -> x2, local copies, waits for them, and re-layouts: 3.99 us -> 1.51 us  [on_device(): ring = [jnp.stack([same[step], other[step]]) for step in (1, 2, 3)]]
    another operation x2 -> x3, other arithmetic: 0.18 us -> 2.32 us  [the longest x2 2.32 us: on_device(): ring = [jnp.stack([same[step], other[step]]) for step in (1, 2, 3)]]
  transfers between devices with their start and end apart: 5 -> 5, of which waited for: 2 -> 1; matrix products, arithmetic and copies ran while one was open for 2% -> 5% of each run, Pallas kernels for 4% -> 4%
where the time goes in v6:
time: 170 us; the launch traced here: 169 us
  blocking collectives  111 us (65%)
  Pallas kernels  32.5 us (19%)
  starting transfers between devices  8.6 us (5%)
  waiting for transfers between devices  6.72 us (4%)
  other arithmetic  4.9 us (3%)
  local copies, waits for them, and re-layouts  4.16 us (2%)
    all_to_all x1, blocking collectives, on_device(): lax.all_to_all(outgoing, 'ping', split_axis=0, concat_axis=0, tiled=True)  64.3 us
    all_to_all x1, blocking collectives, exchange(): lax.all_to_all(blocks, 'ping', split_axis=0, concat_axis=0, tiled=True)  46.5 us
    pallas_call x1, Pallas kernels, form_images(): pl.pallas_call(functools.partial(image_kernel, chunks), grid_spec=pltpu.P...  13.9 us
    pallas_call x2, Pallas kernels, compress(): pl.pallas_call(functools.partial(compress_kernel, relative), grid_spec=pl...  11.1 us
    pallas_call x2, Pallas kernels, pack(): pl.pallas_call(functools.partial(pack_kernel, len(sources) > 1), grid_spe...  7.51 us
    all_to_all x1, waiting for transfers between devices, on_device(): lax.all_to_all(sent, 'band', split_axis=0, concat_axis=0, tiled=True)  6.7 us
    all_to_all x1, starting transfers between devices, on_device(): lax.all_to_all(sent, 'band', split_axis=0, concat_axis=0, tiled=True)  4.7 us
    ppermute x3, starting transfers between devices, on_device(): lax.ppermute(part, 'band', ring_step(step + 1, 0))  3.4 us
  transfers between devices with their start and end apart: 5, of which 1 were waited for; matrix products, arithmetic and copies ran while one was open for 5% of the time, Pallas kernels for 4%

profile of v6, /device:TPU:0, one launch (start us, length us, event | category | flops | bytes accessed | tf_op | source)
XLA Modules:
  0.0 168.7 jit_solution(656707643913829982)
XLA Ops:
  0.0 4.4 %compress.1 = bf16[8,2,8,3,16,128]{5,4,3,2,1,0:T(8,128)(2,1)} custom-call(s32[1]{0:T(128)} %bitcast.1.band_ref, bf16[16,8,128,128]{3,2,1,0:T(8,128)(2,1)} %bitcast.30, bf16[8,2,128]{2,1,0:T(2,128)(2,1)} %taps_ref.3), custom_call_target="tpu_custom_call" | custom-call | tf_op jit(solution)/shard_map/compress/pallas_call | solution.py:67
  4.5 4.7 %all-to-all-start.1 = ((bf16[8,2,8,3,16,128]{5,4,3,2,1,0:T(8,128)(2,1)}), bf16[8,2,8,3,16,128]{5,4,3,2,1,0:T(8,128)(2,1)S(1)}, u32[]{:S(2)}, u32[]{:S(2)}) async-start(bf16[8,2,8,3,16,128]{5,4,3,2,1,0:T(8,128)(2,1)} %compress.1), calls=%async_computation.1 | async-start | bytes 3145728 | tf_op jit(solution)/shard_map/all_to_all | solution.py:257
  9.2 6.7 %compress_relative.1 = (bf16[4,2,8,5,16,128]{5,4,3,2,1,0:T(8,128)(2,1)}, bf16[4,2,8,5,16,128]{5,4,3,2,1,0:T(8,128)(2,1)}) custom-call(s32[1]{0:T(128)} %bitcast.1.band_ref, bf16[16,8,128,128]{3,2,1,0:T(8,128)(2,1)} %bitcast.31, bf16[8,2,128]{2,1,0:T(2,128)(2,1)} %taps_ref.3), custom_call_target="tpu_custom_call" | custom-call | tf_op jit(solution)/shard_map/compress_relative/pallas_call | solution.py:67
  15.9 0.5 collective-permute-start
  16.4 0.1 mul.15
  16.5 0.1 reshape.109
  16.6 0.4 convert_reduce_fusion
  17.0 0.1 select_reduce_fusion
  17.1 0.1 copy.18
  17.2 0.7 sub.7.ids_ref
  17.9 0.2 fusion
  18.2 0.6 fusion.4.table_ref
  18.8 0.7 compare_reduce_fusion
  19.5 0.7 pad_maximum_fusion.3
  20.2 1.3 fusion.5
  21.5 0.0 collective-permute-done
  21.5 0.2 fusion.6
  21.7 1.1 pad_maximum_fusion.2
  22.8 1.2 pad_maximum_fusion
  24.0 6.7 %all-to-all-done.1 = bf16[8,2,8,3,16,128]{5,4,3,2,1,0:T(8,128)(2,1)S(1)} async-done(((bf16[8,2,8,3,16,128]{5,4,3,2,1,0:T(8,128)(2,1)}), bf16[8,2,8,3,16,128]{5,4,3,2,1,0:T(8,128)(2,1)S(1)}, u32[]{:S(2)}, u32[]{:S(2)}) %all-to-all-start.1) | async-done | bytes 1572896 | tf_op jit(solution)/shard_map/all_to_all | solution.py:257
  30.7 1.1 copy-done.1
  31.9 4.1 %pack.2 = bf16[32,8,48,128]{3,2,1,0:T(8,128)(2,1)S(1)} custom-call(s32[16]{0:T(128)} %fusion.4.table_ref, s32[1]{0:T(128)} %bitcast.1.band_ref, bf16[8,2,8,48,128]{4,3,2,1,0:T(8,128)(2,1)} %bitcast.32), custom_call_target="tpu_custom_call" | custom-call | tf_op jit(solution)/shard_map/pack/pallas_call | solution.py:124
  36.0 0.6 collective-permute-start.1
  36.6 2.1 %collective-permute-start.2 = (bf16[2,2,8,5,16,128]{5,4,3,2,1,0:T(8,128)(2,1)}, bf16[2,2,8,5,16,128]{5,4,3,2,1,0:T(8,128)(2,1)}, u32[]{:S(2)}, u32[]{:S(2)}) collective-permute-start(bf16[2,2,8,5,16,128]{5,4,3,2,1,0:T(8,128)(2,1)} %get-tuple-element.31), channel_id=1, source_target_pairs={{0,4},{1,5},{2,6},{3,7},{4,0},{5,1},{6,2},{7,3},{8,12},{9,13},{10,... | collective-permute-start | bytes 1966088 | tf_op jit(solution)/shard_map/ppermute | solution.py:266
  38.7 0.7 collective-permute-start.3
  40.0 47.1 %conditional.1 = (bf16[32,8,48,128]{3,2,1,0:T(8,128)(2,1)S(1)}) conditional(s32[]{:T(128)} %convert_element_type.9, bf16[32,8,48,128]{3,2,1,0:T(8,128)(2,1)S(1)} %pack.2, bf16[32,8,48,128]{3,2,1,0:T(8,128)(2,1)S(1)} %pack.2), branch_computations={%region_3.4_spmd, %region_4.5_spmd} | conditional | bytes 12582920 | solution.py:238
  40.0 0.5 copy.27
  40.6 46.5 %all_to_all.14 = bf16[32,8,48,128]{3,2,1,0:T(8,128)(2,1)S(1)} all-to-all(bf16[32,8,48,128]{3,2,1,0:T(8,128)(2,1)S(1)} %copy.27), channel_id=1, replica_groups=mesh['ping'=16,'band'=8] {'ping'}, dimensions={0} | all-to-all | bytes 6291456 | tf_op jit(solution)/shard_map/cond/branch_1_fun/all_to_all | solution.py:236
  87.1 0.0 collective-permute-done.1
  87.1 3.5 %pack.3 = bf16[32,8,80,128]{3,2,1,0:T(8,128)(2,1)} custom-call(s32[16]{0:T(128)} %fusion.4.table_ref, s32[1]{0:T(128)} %bitcast.1.band_ref, bf16[4,2,8,80,128]{4,3,2,1,0:T(8,128)(2,1)} %bitcast.33, bf16[4,2,8,80,128]{4,3,2,1,0:T(8,128)(2,1)} %bitcast.34, bf16[2,2,8,80,128]{4,3,2,1,0:T(8,128)(2,1)} %bitcast.17.refs_2_, ...), custom_call_target="tpu_custom_call" | custom-call | tf_op jit(solution)/shard_map/pack/pallas_call | solution.py:124
  90.5 64.3 %all_to_all.15.refs_1_ = bf16[32,8,80,128]{3,2,1,0:T(8,128)(2,1)} all-to-all(bf16[32,8,80,128]{3,2,1,0:T(8,128)(2,1)} %pack.3), channel_id=1, replica_groups=mesh['ping'=16,'band'=8] {'ping'}, dimensions={0} | all-to-all | bytes 10485760 | tf_op jit(solution)/shard_map/all_to_all | solution.py:270
  154.8 13.9 %form_images.1 = bf16[2048,1024]{1,0:T(8,128)(2,1)} custom-call(s32[32]{0:T(128)} %sub.7.ids_ref, s32[8]{0:T(128)} %offsets_ref.1, bf16[32,8,48,128]{3,2,1,0:T(8,128)(2,1)S(1)} %get-tuple-element.52.refs_0_, bf16[32,8,80,128]{3,2,1,0:T(8,128)(2,1)} %all_to_all.15.refs_1_, bf16[256,256]{1,0:T(8,128)(2,1)} %bitcast.35, bf16[8,384,128]{2,1,0:T(8,128)(2,1)} %refs_3_.1), custom_call_target="tpu_custom_call" | custom-call | tf_op jit(solution)/shard_map/form_images/pallas_call | solution.py:185
  (24 shorter events, 0.1 us)
Async XLA Ops:
  0.0 17.9 %copy-start = (bf16[2,128,64]{1,2,0:T(8,128)(2,1)S(1)}, bf16[2,128,64]{1,2,0:T(8,128)(2,1)}, u32[]{:S(2)}) copy-start(bf16[2,128,64]{1,2,0:T(8,128)(2,1)} %param.13) | copy-start | bytes 98308
  4.5 11.9 %copy-start.5 = (s32[256]{0:T(256)S(1)}, s32[256]{0:T(256)}, u32[]{:S(2)}) copy-start(s32[256]{0:T(256)} %param.17) | copy-start | bytes 3076
  4.5 12.0 %copy-start.4 = (s32[256]{0:T(256)S(1)}, s32[256]{0:T(256)}, u32[]{:S(2)}) copy-start(s32[256]{0:T(256)} %param.16) | copy-start | bytes 3076
  4.5 13.4 %copy-start.3 = (bf16[2,64,64]{2,1,0:T(8,128)(2,1)S(1)}, bf16[2,64,64]{2,1,0:T(8,128)(2,1)}, u32[]{:S(2)}) copy-start(bf16[2,64,64]{2,1,0:T(8,128)(2,1)} %param.12) | copy-start | bytes 49156
  4.5 26.3 %all-to-all-start.1 = ((bf16[8,2,8,3,16,128]{5,4,3,2,1,0:T(8,128)(2,1)}), bf16[8,2,8,3,16,128]{5,4,3,2,1,0:T(8,128)(2,1)S(1)}, u32[]{:S(2)}, u32[]{:S(2)}) async-start(bf16[8,2,8,3,16,128]{5,4,3,2,1,0:T(8,128)(2,1)} %compress.1), calls=%async_computation.1 | async-start | bytes 3145728 | tf_op jit(solution)/shard_map/all_to_all | solution.py:257
  15.9 5.7 %collective-permute-start = (bf16[4,2,8,5,16,128]{5,4,3,2,1,0:T(8,128)(2,1)}, bf16[4,2,8,5,16,128]{5,4,3,2,1,0:T(8,128)(2,1)S(1)}, u32[]{:S(2)}, u32[]{:S(2)}) collective-permute-start(bf16[4,2,8,5,16,128]{5,4,3,2,1,0:T(8,128)(2,1)} %get-tuple-element.26), channel_id=1, source_target_pairs={{0,1},{1,0},{2,3},{3,2},{4,5},{5,4},{6,7},{7,6},{8,9},{9,8},{10,11... | collective-permute-start | bytes 3932168 | tf_op jit(solution)/shard_map/ppermute | solution.py:259
  21.5 9.2 %copy-start.2 = (bf16[4,2,8,5,16,128]{5,4,3,2,1,0:T(8,128)(2,1)}, bf16[4,2,8,5,16,128]{5,4,3,2,1,0:T(8,128)(2,1)S(1)}, u32[]{:S(2)}) copy-start(bf16[4,2,8,5,16,128]{5,4,3,2,1,0:T(8,128)(2,1)S(1)} %collective-permute-done) | copy-start | bytes 3932164
  30.7 1.1 copy-start.1
  36.0 51.1 %collective-permute-start.1 = (bf16[2,2,8,5,16,128]{5,4,3,2,1,0:T(8,128)(2,1)}, bf16[2,2,8,5,16,128]{5,4,3,2,1,0:T(8,128)(2,1)}, u32[]{:S(2)}, u32[]{:S(2)}) collective-permute-start(bf16[2,2,8,5,16,128]{5,4,3,2,1,0:T(8,128)(2,1)} %get-tuple-element.30), channel_id=1, source_target_pairs={{0,2},{1,3},{2,4},{3,5},{4,6},{5,7},{6,0},{7,1},{8,10},{9,11},{10,... | collective-permute-start | bytes 1966088 | tf_op jit(solution)/shard_map/ppermute | solution.py:266
  36.6 50.5 %collective-permute-start.2 = (bf16[2,2,8,5,16,128]{5,4,3,2,1,0:T(8,128)(2,1)}, bf16[2,2,8,5,16,128]{5,4,3,2,1,0:T(8,128)(2,1)}, u32[]{:S(2)}, u32[]{:S(2)}) collective-permute-start(bf16[2,2,8,5,16,128]{5,4,3,2,1,0:T(8,128)(2,1)} %get-tuple-element.31), channel_id=1, source_target_pairs={{0,4},{1,5},{2,6},{3,7},{4,0},{5,1},{6,2},{7,3},{8,12},{9,13},{10,... | collective-permute-start | bytes 1966088 | tf_op jit(solution)/shard_map/ppermute | solution.py:266
  38.7 48.4 %collective-permute-start.3 = (bf16[2,2,8,5,16,128]{5,4,3,2,1,0:T(8,128)(2,1)}, bf16[2,2,8,5,16,128]{5,4,3,2,1,0:T(8,128)(2,1)}, u32[]{:S(2)}, u32[]{:S(2)}) collective-permute-start(bf16[2,2,8,5,16,128]{5,4,3,2,1,0:T(8,128)(2,1)} %pad_maximum_fusion.2), channel_id=1, source_target_pairs={{0,6},{1,7},{2,0},{3,1},{4,2},{5,3},{6,4},{7,5},{8,14},{9,15},{10,... | collective-permute-start | bytes 1966088 | tf_op jit(solution)/shard_map/ppermute | solution.py:266

commit v7 on v6

--- a/solution.py
+++ b/solution.py
@@ -83,7 +83,7 @@
 
 
 def pack_kernel(relative, table_ref, band_ref, *refs):
-    sources, (out_ref, held, in_sems, out_sems) = refs[:-4], refs[-4:]
+    sources, (out_ref, sems) = refs[:-2], refs[-2:]
 
     def source(block):
         if not relative:
@@ -96,17 +96,11 @@
             return block
         return 2 * band_at(band_ref[0], 4 - block // 4, block // 2 % 2) + block % 2
 
-    def fetch(block):
-        return pltpu.make_async_copy(source(block), held.at[block], in_sems.at[block])
-
     def send(block):
         slot = jnp.maximum(table_ref[name(block)], 0)
-        return pltpu.make_async_copy(held.at[block], out_ref.at[slot], out_sems.at[block])
+        return pltpu.make_async_copy(source(block), out_ref.at[slot], sems.at[block])
 
     for block in range(16):
-        fetch(block).start()
-    for block in range(16):
-        fetch(block).wait()
 
         @pl.when(table_ref[name(block)] >= 0)
         def _():
@@ -121,18 +115,15 @@
 
 def pack(table, band, *sources):
     shape, kind = sources[0].shape[2:], sources[0].dtype
+    sources = [pltpu.with_memory_space_constraint(source, pltpu.VMEM) for source in sources]
     return pl.pallas_call(
         functools.partial(pack_kernel, len(sources) > 1),
         grid_spec=pltpu.PrefetchScalarGridSpec(
             num_scalar_prefetch=2,
             grid=(1,),
-            in_specs=[pl.BlockSpec(memory_space=pl.ANY)] * len(sources),
+            in_specs=[pl.BlockSpec(memory_space=pltpu.VMEM)] * len(sources),
             out_specs=pl.BlockSpec(memory_space=pl.ANY),
-            scratch_shapes=[
-                pltpu.VMEM((16,) + shape, kind),
-                pltpu.SemaphoreType.DMA((16,)),
-                pltpu.SemaphoreType.DMA((16,)),
-            ],
+            scratch_shapes=[pltpu.SemaphoreType.DMA((16,))],
         ),
         out_shape=jax.ShapeDtypeStruct((32,) + shape, kind),
         compiler_params=pltpu.CompilerParams(vmem_limit_bytes=VMEM_LIMIT),
@@ -172,12 +163,14 @@
 
     @pl.when(step >= 4)
     def _():
-        start = offsets_ref[jnp.maximum(step - 4, 0)]
-        for half in range(2):
-            rows = pl.ds(1024 * half, 1024)
-            slab = jnp.concatenate([turned[start + i, rows, :] for i in range(3)], 1)
-            product = jnp.dot(slab, range_ref[0], preferred_element_type=jnp.float32)
-            out_ref[rows, :] = product.astype(jnp.bfloat16)
+        for one in range(2):
+            start = offsets_ref[jnp.maximum(step - 4, 0) * 2 + one]
+            columns = pl.ds(128 * one, 128)
+            for half in range(2):
+                rows = pl.ds(1024 * half, 1024)
+                slab = jnp.concatenate([turned[start + i, rows, :] for i in range(3)], 1)
+                product = jnp.dot(slab, range_ref[one], preferred_element_type=jnp.float32)
+                out_ref[rows, columns] = product.astype(jnp.bfloat16)
 
 
 def form_images(ids, offsets, arrived, angle, range_weights):
@@ -186,16 +179,16 @@
         functools.partial(image_kernel, chunks),
         grid_spec=pltpu.PrefetchScalarGridSpec(
             num_scalar_prefetch=2,
-            grid=(12,),
+            grid=(8,),
             in_specs=[
                 pl.BlockSpec((32, 2, part.shape[2], 128), lambda s, *_: (0, jnp.minimum(s, 3), 0, 0))
                 for part in arrived
             ]
             + [
                 pl.BlockSpec((256, 256), lambda s, *_: (0, 0)),
-                pl.BlockSpec((1, 384, 128), lambda s, *_: (jnp.maximum(s - 4, 0), 0, 0)),
+                pl.BlockSpec((2, 384, 128), lambda s, *_: (jnp.maximum(s - 4, 0), 0, 0)),
             ],
-            out_specs=pl.BlockSpec((2048, 128), lambda s, *_: (0, jnp.maximum(s - 4, 0))),
+            out_specs=pl.BlockSpec((2048, 256), lambda s, *_: (0, jnp.maximum(s - 4, 0))),
             scratch_shapes=[
                 pltpu.VMEM((16, 2, 128, 128), jnp.float32),
                 pltpu.VMEM((8, 2048, 128), jnp.bfloat16),

time: 170 us -> 166 us (0.976)
  Pallas kernels: 32.5 us -> 28.8 us
    pallas_call x1, Pallas kernels: 13.9 us -> 11.9 us  [form_images(): pl.pallas_call(functools.partial(image_kernel, chunks), grid_spec=pltpu.P...]
    pallas_call x2, Pallas kernels: 7.51 us -> 5.79 us  [pack(): pl.pallas_call(functools.partial(pack_kernel, len(sources) > 1), grid_spe...]
  transfers between devices with their start and end apart: 5 -> 5, of which waited for: 1 -> 1; matrix products, arithmetic and copies ran while one was open for 5% -> 4% of each run, Pallas kernels for 4% -> 4%
where the time goes in v7:
time: 166 us
  blocking collectives  111 us (67%)
  Pallas kernels  28.8 us (17%)
  starting transfers between devices  8.6 us (5%)
  waiting for transfers between devices  6.95 us (4%)
  other arithmetic  4.72 us (3%)
  local copies, waits for them, and re-layouts  4.42 us (3%)
    all_to_all x1, blocking collectives, on_device(): lax.all_to_all(outgoing, 'ping', split_axis=0, concat_axis=0, tiled=True)  64.5 us
    all_to_all x1, blocking collectives, exchange(): lax.all_to_all(blocks, 'ping', split_axis=0, concat_axis=0, tiled=True)  46.5 us
    pallas_call x1, Pallas kernels, form_images(): pl.pallas_call(functools.partial(image_kernel, chunks), grid_spec=pltpu.P...  11.9 us
    pallas_call x2, Pallas kernels, compress(): pl.pallas_call(functools.partial(compress_kernel, relative), grid_spec=pl...  11.1 us
    all_to_all x1, waiting for transfers between devices, on_device(): lax.all_to_all(sent, 'band', split_axis=0, concat_axis=0, tiled=True)  6.94 us
    pallas_call x2, Pallas kernels, pack(): pl.pallas_call(functools.partial(pack_kernel, len(sources) > 1), grid_spe...  5.79 us
    all_to_all x1, starting transfers between devices, on_device(): lax.all_to_all(sent, 'band', split_axis=0, concat_axis=0, tiled=True)  4.7 us
    ppermute x3, starting transfers between devices, on_device(): lax.ppermute(part, 'band', ring_step(step + 1, 0))  3.4 us
  transfers between devices with their start and end apart: 5, of which 1 were waited for; matrix products, arithmetic and copies ran while one was open for 4% of the time, Pallas kernels for 4%

profile of v7, /device:TPU:0, one launch (start us, length us, event | category | flops | bytes accessed | tf_op | source)
XLA Modules:
  0.0 165.6 jit_solution(470889754588905357)
XLA Ops:
  0.0 4.4 %compress.1 = bf16[8,2,8,3,16,128]{5,4,3,2,1,0:T(8,128)(2,1)} custom-call(s32[1]{0:T(128)} %bitcast.1.band_ref, bf16[16,8,128,128]{3,2,1,0:T(8,128)(2,1)} %bitcast.33, bf16[8,2,128]{2,1,0:T(2,128)(2,1)} %taps_ref.3), custom_call_target="tpu_custom_call" | custom-call | tf_op jit(solution)/shard_map/compress/pallas_call | solution.py:67
  4.5 4.7 %all-to-all-start.1 = ((bf16[8,2,8,3,16,128]{5,4,3,2,1,0:T(8,128)(2,1)}), bf16[8,2,8,3,16,128]{5,4,3,2,1,0:T(8,128)(2,1)S(1)}, u32[]{:S(2)}, u32[]{:S(2)}) async-start(bf16[8,2,8,3,16,128]{5,4,3,2,1,0:T(8,128)(2,1)} %compress.1), calls=%async_computation.1 | async-start | bytes 3145728 | tf_op jit(solution)/shard_map/all_to_all | solution.py:250
  9.2 6.7 %compress_relative.1 = (bf16[4,2,8,5,16,128]{5,4,3,2,1,0:T(8,128)(2,1)}, bf16[4,2,8,5,16,128]{5,4,3,2,1,0:T(8,128)(2,1)}) custom-call(s32[1]{0:T(128)} %bitcast.1.band_ref, bf16[16,8,128,128]{3,2,1,0:T(8,128)(2,1)} %bitcast.34, bf16[8,2,128]{2,1,0:T(2,128)(2,1)} %taps_ref.3), custom_call_target="tpu_custom_call" | custom-call | tf_op jit(solution)/shard_map/compress_relative/pallas_call | solution.py:67
  15.9 0.5 collective-permute-start
  16.4 0.1 mul.15
  16.5 0.1 reshape.109
  16.6 0.4 convert_reduce_fusion
  17.0 0.1 select_reduce_fusion
  17.1 0.1 copy.18
  17.2 0.6 sub.7.ids_ref
  17.9 0.2 fusion
  18.2 0.6 fusion.4.table_ref
  18.7 0.7 compare_reduce_fusion
  19.4 0.7 pad_maximum_fusion.3
  20.1 1.3 fusion.5
  21.5 0.0 collective-permute-done
  21.5 0.2 fusion.6
  21.7 0.9 pad_maximum_fusion.2
  22.6 1.2 pad_maximum_fusion
  23.8 6.9 %all-to-all-done.1 = bf16[8,2,8,3,16,128]{5,4,3,2,1,0:T(8,128)(2,1)S(1)} async-done(((bf16[8,2,8,3,16,128]{5,4,3,2,1,0:T(8,128)(2,1)}), bf16[8,2,8,3,16,128]{5,4,3,2,1,0:T(8,128)(2,1)S(1)}, u32[]{:S(2)}, u32[]{:S(2)}) %all-to-all-start.1) | async-done | bytes 1572896 | tf_op jit(solution)/shard_map/all_to_all | solution.py:250
  30.7 2.0 %pack.2 = bf16[32,8,48,128]{3,2,1,0:T(8,128)(2,1)} custom-call(s32[16]{0:T(128)} %fusion.4.table_ref, s32[1]{0:T(128)} %bitcast.1.band_ref, bf16[8,2,8,48,128]{4,3,2,1,0:T(8,128)(2,1)S(1)} %bitcast.30), custom_call_target="tpu_custom_call" | custom-call | tf_op jit(solution)/shard_map/pack/pallas_call | solution.py:119
  32.8 0.6 collective-permute-start.1
  33.4 2.1 %collective-permute-start.2 = (bf16[2,2,8,5,16,128]{5,4,3,2,1,0:T(8,128)(2,1)}, bf16[2,2,8,5,16,128]{5,4,3,2,1,0:T(8,128)(2,1)}, u32[]{:S(2)}, u32[]{:S(2)}) collective-permute-start(bf16[2,2,8,5,16,128]{5,4,3,2,1,0:T(8,128)(2,1)} %get-tuple-element.31), channel_id=1, source_target_pairs={{0,4},{1,5},{2,6},{3,7},{4,0},{5,1},{6,2},{7,3},{8,12},{9,13},{10,... | collective-permute-start | bytes 1966088 | tf_op jit(solution)/shard_map/ppermute | solution.py:259
  35.5 0.7 collective-permute-start.3
  36.9 48.5 %conditional.1 = (bf16[32,8,48,128]{3,2,1,0:T(8,128)(2,1)}) conditional(s32[]{:T(128)} %convert_element_type.9, bf16[32,8,48,128]{3,2,1,0:T(8,128)(2,1)} %pack.2, bf16[32,8,48,128]{3,2,1,0:T(8,128)(2,1)} %pack.2), branch_computations={%region_3.4_spmd, %region_4.5_spmd} | conditional | bytes 18874404 | solution.py:231
  36.9 2.0 %copy-done.3 = bf16[32,8,48,128]{3,2,1,0:T(8,128)(2,1)S(1)} copy-done((bf16[32,8,48,128]{3,2,1,0:T(8,128)(2,1)S(1)}, bf16[32,8,48,128]{3,2,1,0:T(8,128)(2,1)}, u32[]{:S(2)}) %copy-start.3) | copy-done | bytes 3145752 | tf_op jit(solution)/shard_map/cond
  38.9 46.5 %all_to_all.14 = bf16[32,8,48,128]{3,2,1,0:T(8,128)(2,1)} all-to-all(bf16[32,8,48,128]{3,2,1,0:T(8,128)(2,1)S(1)} %copy-done.3), channel_id=1, replica_groups=mesh['ping'=16,'band'=8] {'ping'}, dimensions={0} | all-to-all | bytes 6291456 | tf_op jit(solution)/shard_map/cond/branch_1_fun/all_to_all | solution.py:229
  85.4 0.0 collective-permute-done.1
  85.4 0.0 collective-permute-done.2
  85.4 3.7 %pack.3 = bf16[32,8,80,128]{3,2,1,0:T(8,128)(2,1)} custom-call(s32[16]{0:T(128)} %fusion.4.table_ref, s32[1]{0:T(128)} %bitcast.1.band_ref, bf16[4,2,8,80,128]{4,3,2,1,0:T(8,128)(2,1)S(1)} %bitcast.31, bf16[4,2,8,80,128]{4,3,2,1,0:T(8,128)(2,1)S(1)} %bitcast.32, bf16[2,2,8,80,128]{4,3,2,1,0:T(8,128)(2,1)} %bitcast.17.refs_2_, ...), custom_call_target="tpu_custom_call" | custom-call | tf_op jit(solution)/shard_map/pack/pallas_call | solution.py:119
  89.2 64.5 %all_to_all.15.refs_1_ = bf16[32,8,80,128]{3,2,1,0:T(8,128)(2,1)} all-to-all(bf16[32,8,80,128]{3,2,1,0:T(8,128)(2,1)} %pack.3), channel_id=1, replica_groups=mesh['ping'=16,'band'=8] {'ping'}, dimensions={0} | all-to-all | bytes 10485760 | tf_op jit(solution)/shard_map/all_to_all | solution.py:263
  153.7 11.9 %form_images.1 = bf16[2048,1024]{1,0:T(8,128)(2,1)} custom-call(s32[32]{0:T(128)} %sub.7.ids_ref, s32[8]{0:T(128)} %offsets_ref.1, bf16[32,8,48,128]{3,2,1,0:T(8,128)(2,1)S(1)} %copy-done.2, bf16[32,8,80,128]{3,2,1,0:T(8,128)(2,1)} %all_to_all.15.refs_1_, bf16[256,256]{1,0:T(8,128)(2,1)} %bitcast.35, bf16[8,384,128]{2,1,0:T(8,128)(2,1)} %refs_3_.1), custom_call_target="tpu_custom_call" | custom-call | tf_op jit(solution)/shard_map/form_images/pallas_call | solution.py:178
  (25 shorter events, 0.1 us)
Async XLA Ops:
  0.0 17.8 %copy-start = (bf16[2,128,64]{1,2,0:T(8,128)(2,1)S(1)}, bf16[2,128,64]{1,2,0:T(8,128)(2,1)}, u32[]{:S(2)}) copy-start(bf16[2,128,64]{1,2,0:T(8,128)(2,1)} %param.13) | copy-start | bytes 98308
  4.5 11.9 %copy-start.6 = (s32[256]{0:T(256)S(1)}, s32[256]{0:T(256)}, u32[]{:S(2)}) copy-start(s32[256]{0:T(256)} %param.17) | copy-start | bytes 3076
  4.5 12.0 %copy-start.5 = (s32[256]{0:T(256)S(1)}, s32[256]{0:T(256)}, u32[]{:S(2)}) copy-start(s32[256]{0:T(256)} %param.16) | copy-start | bytes 3076
  4.5 13.4 %copy-start.4 = (bf16[2,64,64]{2,1,0:T(8,128)(2,1)S(1)}, bf16[2,64,64]{2,1,0:T(8,128)(2,1)}, u32[]{:S(2)}) copy-start(bf16[2,64,64]{2,1,0:T(8,128)(2,1)} %param.12) | copy-start | bytes 49156
  4.5 26.3 %all-to-all-start.1 = ((bf16[8,2,8,3,16,128]{5,4,3,2,1,0:T(8,128)(2,1)}), bf16[8,2,8,3,16,128]{5,4,3,2,1,0:T(8,128)(2,1)S(1)}, u32[]{:S(2)}, u32[]{:S(2)}) async-start(bf16[8,2,8,3,16,128]{5,4,3,2,1,0:T(8,128)(2,1)} %compress.1), calls=%async_computation.1 | async-start | bytes 3145728 | tf_op jit(solution)/shard_map/all_to_all | solution.py:250
  15.9 5.6 %collective-permute-start = (bf16[4,2,8,5,16,128]{5,4,3,2,1,0:T(8,128)(2,1)}, bf16[4,2,8,5,16,128]{5,4,3,2,1,0:T(8,128)(2,1)S(1)}, u32[]{:S(2)}, u32[]{:S(2)}) collective-permute-start(bf16[4,2,8,5,16,128]{5,4,3,2,1,0:T(8,128)(2,1)} %get-tuple-element.26), channel_id=1, source_target_pairs={{0,1},{1,0},{2,3},{3,2},{4,5},{5,4},{6,7},{7,6},{8,9},{9,8},{10,11... | collective-permute-start | bytes 3932168 | tf_op jit(solution)/shard_map/ppermute | solution.py:252
  32.8 52.6 %collective-permute-start.1 = (bf16[2,2,8,5,16,128]{5,4,3,2,1,0:T(8,128)(2,1)}, bf16[2,2,8,5,16,128]{5,4,3,2,1,0:T(8,128)(2,1)}, u32[]{:S(2)}, u32[]{:S(2)}) collective-permute-start(bf16[2,2,8,5,16,128]{5,4,3,2,1,0:T(8,128)(2,1)} %get-tuple-element.30), channel_id=1, source_target_pairs={{0,2},{1,3},{2,4},{3,5},{4,6},{5,7},{6,0},{7,1},{8,10},{9,11},{10,... | collective-permute-start | bytes 1966088 | tf_op jit(solution)/shard_map/ppermute | solution.py:259
  33.4 52.0 %collective-permute-start.2 = (bf16[2,2,8,5,16,128]{5,4,3,2,1,0:T(8,128)(2,1)}, bf16[2,2,8,5,16,128]{5,4,3,2,1,0:T(8,128)(2,1)}, u32[]{:S(2)}, u32[]{:S(2)}) collective-permute-start(bf16[2,2,8,5,16,128]{5,4,3,2,1,0:T(8,128)(2,1)} %get-tuple-element.31), channel_id=1, source_target_pairs={{0,4},{1,5},{2,6},{3,7},{4,0},{5,1},{6,2},{7,3},{8,12},{9,13},{10,... | collective-permute-start | bytes 1966088 | tf_op jit(solution)/shard_map/ppermute | solution.py:259
  35.5 49.9 %collective-permute-start.3 = (bf16[2,2,8,5,16,128]{5,4,3,2,1,0:T(8,128)(2,1)}, bf16[2,2,8,5,16,128]{5,4,3,2,1,0:T(8,128)(2,1)}, u32[]{:S(2)}, u32[]{:S(2)}) collective-permute-start(bf16[2,2,8,5,16,128]{5,4,3,2,1,0:T(8,128)(2,1)} %pad_maximum_fusion.2), channel_id=1, source_target_pairs={{0,6},{1,7},{2,0},{3,1},{4,2},{5,3},{6,4},{7,5},{8,14},{9,15},{10,... | collective-permute-start | bytes 1966088 | tf_op jit(solution)/shard_map/ppermute | solution.py:259
  36.9 48.6 %copy-start.1 = (bf16[4,2,8,5,16,128]{5,4,3,2,1,0:T(8,128)(2,1)S(1)}, bf16[4,2,8,5,16,128]{5,4,3,2,1,0:T(8,128)(2,1)}, u32[]{:S(2)}) copy-start(bf16[4,2,8,5,16,128]{5,4,3,2,1,0:T(8,128)(2,1)} %get-tuple-element.34) | copy-start | bytes 3932164
  36.9 2.0 %copy-start.3 = (bf16[32,8,48,128]{3,2,1,0:T(8,128)(2,1)S(1)}, bf16[32,8,48,128]{3,2,1,0:T(8,128)(2,1)}, u32[]{:S(2)}) copy-start(bf16[32,8,48,128]{3,2,1,0:T(8,128)(2,1)} %param.1) | copy-start | bytes 9437188 | tf_op jit(solution)/shard_map/cond
  89.2 64.5 %copy-start.2 = (bf16[32,8,48,128]{3,2,1,0:T(8,128)(2,1)S(1)}, bf16[32,8,48,128]{3,2,1,0:T(8,128)(2,1)}, u32[]{:S(2)}) copy-start(bf16[32,8,48,128]{3,2,1,0:T(8,128)(2,1)} %get-tuple-element.52.refs_0_) | copy-start | bytes 9437188

commit v8 on v7

--- a/solution.py
+++ b/solution.py
@@ -224,11 +224,14 @@
     return table, ids.reshape(32)
 
 
-def to_owners(some, outgoing):
-    def exchange(blocks):
-        return lax.all_to_all(blocks, "ping", split_axis=0, concat_axis=0, tiled=True)
-
-    return lax.cond(some, exchange, lambda blocks: blocks, outgoing)
+def to_owners(some, table, band, source):
+    def exchange(table, band, source):
+        return lax.all_to_all(pack(table, band, source), "ping", split_axis=0, concat_axis=0, tiled=True)
+
+    def nothing(table, band, source):
+        return jnp.zeros((32,) + source.shape[2:], source.dtype)
+
+    return lax.cond(some, exchange, nothing, table, band, source)
 
 
 def flat(part):
@@ -251,13 +254,12 @@
     same, other = compress(band, x, replica, SPLIT, 8 - SPLIT, True)
     other = lax.ppermute(other, "band", ring_step(0, 1))
     ring = [jnp.stack([same[step], other[step]]) for step in (1, 2, 3)]
-    outgoing = pack(table, band, flat(band_tile))
     some = jnp.any(merge_owner >= 0)
-    outgoing, ids, angle, some, same, other, *ring = lax.optimization_barrier(
-        (outgoing, ids, angle, some, same, other, *ring)
+    band_tile, table, ids, angle, some, same, other, *ring = lax.optimization_barrier(
+        (band_tile, table, ids, angle, some, same, other, *ring)
     )
     ring = [lax.ppermute(part, "band", ring_step(step + 1, 0)) for step, part in enumerate(ring)]
-    first = to_owners(some, outgoing)
+    first = to_owners(some, table, band, flat(band_tile))
     first, *ring = lax.optimization_barrier((first, *ring))
     outgoing = pack(table, band, *[flat(part) for part in (same, other, *ring)])
     second = lax.all_to_all(outgoing, "ping", split_axis=0, concat_axis=0, tiled=True)

time: 166 us -> 165 us (level)
    cond x2 -> x0, local copies, waits for them, and re-layouts: 1.98 us -> none
  transfers between devices with their start and end apart: 5 -> 5, of which waited for: 1 -> 1; matrix products, arithmetic and copies ran while one was open for 4% -> 4% of each run, Pallas kernels for 4% -> 5%
where the time goes in v8:
time: 165 us
  blocking collectives  111 us (67%)
  Pallas kernels  28.3 us (17%)
  starting transfers between devices  8.43 us (5%)
  waiting for transfers between devices  7.52 us (5%)
  other arithmetic  4.21 us (3%)
  local copies, waits for them, and re-layouts  3.71 us (2%)
    all_to_all x1, blocking collectives, on_device(): lax.all_to_all(outgoing, 'ping', split_axis=0, concat_axis=0, tiled=True)  64.5 us
    all_to_all x1, blocking collectives, exchange(): lax.all_to_all(pack(table, band, source), 'ping', split_axis=0, concat_ax...  46.8 us
    pallas_call x1, Pallas kernels, form_images(): pl.pallas_call(functools.partial(image_kernel, chunks), grid_spec=pltpu.P...  11.9 us
    pallas_call x2, Pallas kernels, compress(): pl.pallas_call(functools.partial(compress_kernel, relative), grid_spec=pl...  11.1 us
    all_to_all x1, waiting for transfers between devices, on_device(): lax.all_to_all(sent, 'band', split_axis=0, concat_axis=0, tiled=True)  7.51 us
    pallas_call x2, Pallas kernels, pack(): pl.pallas_call(functools.partial(pack_kernel, len(sources) > 1), grid_spe...  5.27 us
    all_to_all x1, starting transfers between devices, on_device(): lax.all_to_all(sent, 'band', split_axis=0, concat_axis=0, tiled=True)  4.7 us
  transfers between devices with their start and end apart: 5, of which 1 were waited for; matrix products, arithmetic and copies ran while one was open for 4% of the time, Pallas kernels for 5%

profile of v8, /device:TPU:0, one launch (start us, length us, event | category | flops | bytes accessed | tf_op | source)
XLA Modules:
  0.0 164.6 jit_solution(17190745356244087877)
XLA Ops:
  0.0 4.4 %compress.1 = bf16[8,2,8,3,16,128]{5,4,3,2,1,0:T(8,128)(2,1)} custom-call(s32[1]{0:T(128)} %bitcast.1.band_ref, bf16[16,8,128,128]{3,2,1,0:T(8,128)(2,1)} %bitcast.33, bf16[8,2,128]{2,1,0:T(2,128)(2,1)} %taps_ref.3), custom_call_target="tpu_custom_call" | custom-call | tf_op jit(solution)/shard_map/compress/pallas_call | solution.py:67
  4.5 4.7 %all-to-all-start.1 = ((bf16[8,2,8,3,16,128]{5,4,3,2,1,0:T(8,128)(2,1)}), bf16[8,2,8,3,16,128]{5,4,3,2,1,0:T(8,128)(2,1)S(1)}, u32[]{:S(2)}, u32[]{:S(2)}) async-start(bf16[8,2,8,3,16,128]{5,4,3,2,1,0:T(8,128)(2,1)} %compress.1), calls=%async_computation.1 | async-start | bytes 3145728 | tf_op jit(solution)/shard_map/all_to_all | solution.py:253
  9.2 6.7 %compress_relative.1 = (bf16[4,2,8,5,16,128]{5,4,3,2,1,0:T(8,128)(2,1)}, bf16[4,2,8,5,16,128]{5,4,3,2,1,0:T(8,128)(2,1)}) custom-call(s32[1]{0:T(128)} %bitcast.1.band_ref, bf16[16,8,128,128]{3,2,1,0:T(8,128)(2,1)} %bitcast.34, bf16[8,2,128]{2,1,0:T(2,128)(2,1)} %taps_ref.3), custom_call_target="tpu_custom_call" | custom-call | tf_op jit(solution)/shard_map/compress_relative/pallas_call | solution.py:67
  15.8 0.5 collective-permute-start
  16.4 0.1 mul.15
  16.4 0.1 reshape.113
  16.5 0.4 convert_reduce_fusion
  17.0 0.1 select_reduce_fusion
  17.1 0.1 copy.18
  17.2 0.6 sub.7.ids_ref
  17.8 0.2 fusion
  18.1 0.7 compare_reduce_fusion
  18.8 0.7 pad_maximum_fusion.3
  19.4 1.3 fusion.5
  20.8 0.0 collective-permute-done
  20.8 0.2 fusion.6
  21.0 1.1 pad_maximum_fusion.2
  22.0 1.2 pad_maximum_fusion
  23.2 7.5 %all-to-all-done.1 = bf16[8,2,8,3,16,128]{5,4,3,2,1,0:T(8,128)(2,1)S(1)} async-done(((bf16[8,2,8,3,16,128]{5,4,3,2,1,0:T(8,128)(2,1)}), bf16[8,2,8,3,16,128]{5,4,3,2,1,0:T(8,128)(2,1)S(1)}, u32[]{:S(2)}, u32[]{:S(2)}) %all-to-all-start.1) | async-done | bytes 1572896 | tf_op jit(solution)/shard_map/all_to_all | solution.py:253
  30.7 0.6 collective-permute-start.1
  31.3 2.1 %collective-permute-start.2 = (bf16[2,2,8,5,16,128]{5,4,3,2,1,0:T(8,128)(2,1)}, bf16[2,2,8,5,16,128]{5,4,3,2,1,0:T(8,128)(2,1)}, u32[]{:S(2)}, u32[]{:S(2)}) collective-permute-start(bf16[2,2,8,5,16,128]{5,4,3,2,1,0:T(8,128)(2,1)} %get-tuple-element.41), channel_id=1, source_target_pairs={{0,4},{1,5},{2,6},{3,7},{4,0},{5,1},{6,2},{7,3},{8,12},{9,13},{10,... | collective-permute-start | bytes 1966088 | tf_op jit(solution)/shard_map/ppermute | solution.py:261
  33.4 0.6 collective-permute-start.3
  34.6 48.6 %conditional.1 = (bf16[32,8,48,128]{3,2,1,0:T(8,128)(2,1)}) conditional(s32[]{:T(128)} %convert_element_type.9, () %tuple.14, (bf16[8,2,8,3,16,128]{5,4,3,2,1,0:T(8,128)(2,1)S(1)}, s32[16]{0:T(128)S(1)}, s32[1]{0:T(128)}) %tuple.15), branch_computations={%region_3.4_spmd, %region_4.5_spmd} | conditional | bytes 6291464 | solution.py:234
  34.7 1.7 %pack.2 = bf16[32,8,48,128]{3,2,1,0:T(8,128)(2,1)} custom-call(s32[16]{0:T(128)S(1)} %get-tuple-element.15.table_ref, s32[1]{0:T(128)} %get-tuple-element.16.band_ref, bf16[8,2,8,48,128]{4,3,2,1,0:T(8,128)(2,1)S(1)} %bitcast.30), custom_call_target="tpu_custom_call" | custom-call | tf_op jit(solution)/shard_map/cond/branch_1_fun/pack/pallas_call | solution.py:119
  36.4 46.8 %all_to_all.14 = bf16[32,8,48,128]{3,2,1,0:T(8,128)(2,1)} all-to-all(bf16[32,8,48,128]{3,2,1,0:T(8,128)(2,1)} %pack.2), channel_id=1, replica_groups=mesh['ping'=16,'band'=8] {'ping'}, dimensions={0} | all-to-all | bytes 6291456 | tf_op jit(solution)/shard_map/cond/branch_1_fun/all_to_all | solution.py:229
  83.2 0.0 collective-permute-done.1
  83.2 0.0 collective-permute-done.2
  83.2 0.0 collective-permute-done.3
  83.3 1.3 copy-done.3
  84.6 3.5 %pack.3 = bf16[32,8,80,128]{3,2,1,0:T(8,128)(2,1)} custom-call(s32[16]{0:T(128)S(1)} %fusion.4.table_ref, s32[1]{0:T(128)} %bitcast.1.band_ref, bf16[4,2,8,80,128]{4,3,2,1,0:T(8,128)(2,1)S(1)} %bitcast.31, bf16[4,2,8,80,128]{4,3,2,1,0:T(8,128)(2,1)S(1)} %bitcast.32, bf16[2,2,8,80,128]{4,3,2,1,0:T(8,128)(2,1)} %bitcast.17.refs_2_, ...), custom_call_target="tpu_custom_call" | custom-call | tf_op jit(solution)/shard_map/pack/pallas_call | solution.py:119
  88.1 64.5 %all_to_all.15.refs_1_ = bf16[32,8,80,128]{3,2,1,0:T(8,128)(2,1)} all-to-all(bf16[32,8,80,128]{3,2,1,0:T(8,128)(2,1)} %pack.3), channel_id=1, replica_groups=mesh['ping'=16,'band'=8] {'ping'}, dimensions={0} | all-to-all | bytes 10485760 | tf_op jit(solution)/shard_map/all_to_all | solution.py:265
  152.6 11.9 %form_images.1 = bf16[2048,1024]{1,0:T(8,128)(2,1)} custom-call(s32[32]{0:T(128)} %sub.7.ids_ref, s32[8]{0:T(128)} %offsets_ref.1, bf16[32,8,48,128]{3,2,1,0:T(8,128)(2,1)S(1)} %copy-done.4, bf16[32,8,80,128]{3,2,1,0:T(8,128)(2,1)} %all_to_all.15.refs_1_, bf16[256,256]{1,0:T(8,128)(2,1)} %bitcast.35, bf16[8,384,128]{2,1,0:T(8,128)(2,1)} %refs_3_.1), custom_call_target="tpu_custom_call" | custom-call | tf_op jit(solution)/shard_map/form_images/pallas_call | solution.py:178
  (27 shorter events, 0.1 us)
Async XLA Ops:
  0.0 17.8 %copy-start = (bf16[2,128,64]{1,2,0:T(8,128)(2,1)S(1)}, bf16[2,128,64]{1,2,0:T(8,128)(2,1)}, u32[]{:S(2)}) copy-start(bf16[2,128,64]{1,2,0:T(8,128)(2,1)} %param.13) | copy-start | bytes 98308
  4.5 11.9 %copy-start.7 = (s32[256]{0:T(256)S(1)}, s32[256]{0:T(256)}, u32[]{:S(2)}) copy-start(s32[256]{0:T(256)} %param.17) | copy-start | bytes 3076
  4.5 12.0 %copy-start.6 = (s32[256]{0:T(256)S(1)}, s32[256]{0:T(256)}, u32[]{:S(2)}) copy-start(s32[256]{0:T(256)} %param.16) | copy-start | bytes 3076
  4.5 13.3 %copy-start.5 = (bf16[2,64,64]{2,1,0:T(8,128)(2,1)S(1)}, bf16[2,64,64]{2,1,0:T(8,128)(2,1)}, u32[]{:S(2)}) copy-start(bf16[2,64,64]{2,1,0:T(8,128)(2,1)} %param.12) | copy-start | bytes 49156
  4.5 26.3 %all-to-all-start.1 = ((bf16[8,2,8,3,16,128]{5,4,3,2,1,0:T(8,128)(2,1)}), bf16[8,2,8,3,16,128]{5,4,3,2,1,0:T(8,128)(2,1)S(1)}, u32[]{:S(2)}, u32[]{:S(2)}) async-start(bf16[8,2,8,3,16,128]{5,4,3,2,1,0:T(8,128)(2,1)} %compress.1), calls=%async_computation.1 | async-start | bytes 3145728 | tf_op jit(solution)/shard_map/all_to_all | solution.py:253
  15.8 4.9 %collective-permute-start = (bf16[4,2,8,5,16,128]{5,4,3,2,1,0:T(8,128)(2,1)}, bf16[4,2,8,5,16,128]{5,4,3,2,1,0:T(8,128)(2,1)S(1)}, u32[]{:S(2)}, u32[]{:S(2)}) collective-permute-start(bf16[4,2,8,5,16,128]{5,4,3,2,1,0:T(8,128)(2,1)} %get-tuple-element.35), channel_id=1, source_target_pairs={{0,1},{1,0},{2,3},{3,2},{4,5},{5,4},{6,7},{7,6},{8,9},{9,8},{10,11... | collective-permute-start | bytes 3932168 | tf_op jit(solution)/shard_map/ppermute | solution.py:255
  20.8 13.8 %copy-start.2 = (bf16[4,2,8,5,16,128]{5,4,3,2,1,0:T(8,128)(2,1)}, bf16[4,2,8,5,16,128]{5,4,3,2,1,0:T(8,128)(2,1)S(1)}, u32[]{:S(2)}) copy-start(bf16[4,2,8,5,16,128]{5,4,3,2,1,0:T(8,128)(2,1)S(1)} %collective-permute-done) | copy-start | bytes 3932164
  30.7 52.5 %collective-permute-start.1 = (bf16[2,2,8,5,16,128]{5,4,3,2,1,0:T(8,128)(2,1)}, bf16[2,2,8,5,16,128]{5,4,3,2,1,0:T(8,128)(2,1)}, u32[]{:S(2)}, u32[]{:S(2)}) collective-permute-start(bf16[2,2,8,5,16,128]{5,4,3,2,1,0:T(8,128)(2,1)} %get-tuple-element.40), channel_id=1, source_target_pairs={{0,2},{1,3},{2,4},{3,5},{4,6},{5,7},{6,0},{7,1},{8,10},{9,11},{10,... | collective-permute-start | bytes 1966088 | tf_op jit(solution)/shard_map/ppermute | solution.py:261
  31.3 51.9 %collective-permute-start.2 = (bf16[2,2,8,5,16,128]{5,4,3,2,1,0:T(8,128)(2,1)}, bf16[2,2,8,5,16,128]{5,4,3,2,1,0:T(8,128)(2,1)}, u32[]{:S(2)}, u32[]{:S(2)}) collective-permute-start(bf16[2,2,8,5,16,128]{5,4,3,2,1,0:T(8,128)(2,1)} %get-tuple-element.41), channel_id=1, source_target_pairs={{0,4},{1,5},{2,6},{3,7},{4,0},{5,1},{6,2},{7,3},{8,12},{9,13},{10,... | collective-permute-start | bytes 1966088 | tf_op jit(solution)/shard_map/ppermute | solution.py:261
  33.4 49.9 %collective-permute-start.3 = (bf16[2,2,8,5,16,128]{5,4,3,2,1,0:T(8,128)(2,1)}, bf16[2,2,8,5,16,128]{5,4,3,2,1,0:T(8,128)(2,1)}, u32[]{:S(2)}, u32[]{:S(2)}) collective-permute-start(bf16[2,2,8,5,16,128]{5,4,3,2,1,0:T(8,128)(2,1)} %pad_maximum_fusion.2), channel_id=1, source_target_pairs={{0,6},{1,7},{2,0},{3,1},{4,2},{5,3},{6,4},{7,5},{8,14},{9,15},{10,... | collective-permute-start | bytes 1966088 | tf_op jit(solution)/shard_map/ppermute | solution.py:261
  34.6 48.6 %copy-start.1 = (bf16[4,2,8,5,16,128]{5,4,3,2,1,0:T(8,128)(2,1)S(1)}, bf16[4,2,8,5,16,128]{5,4,3,2,1,0:T(8,128)(2,1)}, u32[]{:S(2)}) copy-start(bf16[4,2,8,5,16,128]{5,4,3,2,1,0:T(8,128)(2,1)} %get-tuple-element.44) | copy-start | bytes 3932164
  83.3 1.3 copy-start.3
  88.1 64.5 %copy-start.4 = (bf16[32,8,48,128]{3,2,1,0:T(8,128)(2,1)S(1)}, bf16[32,8,48,128]{3,2,1,0:T(8,128)(2,1)}, u32[]{:S(2)}) copy-start(bf16[32,8,48,128]{3,2,1,0:T(8,128)(2,1)} %get-tuple-element.62.refs_0_) | copy-start | bytes 9437188

commit v9 on v8

--- a/solution.py
+++ b/solution.py
@@ -254,6 +254,7 @@
     same, other = compress(band, x, replica, SPLIT, 8 - SPLIT, True)
     other = lax.ppermute(other, "band", ring_step(0, 1))
     ring = [jnp.stack([same[step], other[step]]) for step in (1, 2, 3)]
+    same, other = same[:1], other[:1]
     some = jnp.any(merge_owner >= 0)
     band_tile, table, ids, angle, some, same, other, *ring = lax.optimization_barrier(
         (band_tile, table, ids, angle, some, same, other, *ring)

time: 165 us -> 164 us (level)
  transfers between devices with their start and end apart: 5 -> 5, of which waited for: 1 -> 1; matrix products, arithmetic and copies ran while one was open for 4% -> 5% of each run, Pallas kernels for 5% -> 5%
where the time goes in v9:
time: 164 us; the launch traced here: 163 us
  blocking collectives  111 us (68%)
  Pallas kernels  28.2 us (17%)
  starting transfers between devices  8.44 us (5%)
  waiting for transfers between devices  5.99 us (4%)
  other arithmetic  4.16 us (3%)
  local copies, waits for them, and re-layouts  3.98 us (2%)
    all_to_all x1, blocking collectives, on_device(): lax.all_to_all(outgoing, 'ping', split_axis=0, concat_axis=0, tiled=True)  64.5 us
    all_to_all x1, blocking collectives, exchange(): lax.all_to_all(pack(table, band, source), 'ping', split_axis=0, concat_ax...  46.8 us
    pallas_call x1, Pallas kernels, form_images(): pl.pallas_call(functools.partial(image_kernel, chunks), grid_spec=pltpu.P...  11.9 us
    pallas_call x2, Pallas kernels, compress(): pl.pallas_call(functools.partial(compress_kernel, relative), grid_spec=pl...  11.1 us
    all_to_all x1, waiting for transfers between devices, on_device(): lax.all_to_all(sent, 'band', split_axis=0, concat_axis=0, tiled=True)  5.98 us
    pallas_call x2, Pallas kernels, pack(): pl.pallas_call(functools.partial(pack_kernel, len(sources) > 1), grid_spe...  5.22 us
    all_to_all x1, starting transfers between devices, on_device(): lax.all_to_all(sent, 'band', split_axis=0, concat_axis=0, tiled=True)  4.7 us
  transfers between devices with their start and end apart: 5, of which 1 were waited for; matrix products, arithmetic and copies ran while one was open for 5% of the time, Pallas kernels for 5%

profile of v9, /device:TPU:0, one launch (start us, length us, event | category | flops | bytes accessed | tf_op | source)
XLA Modules:
  0.0 163.1 jit_solution(11307514572912178102)
XLA Ops:
  0.0 0.0 copy-start
  0.0 4.4 %compress.1 = bf16[8,2,8,3,16,128]{5,4,3,2,1,0:T(8,128)(2,1)} custom-call(s32[1]{0:T(128)} %bitcast.1.band_ref, bf16[16,8,128,128]{3,2,1,0:T(8,128)(2,1)} %bitcast.34, bf16[8,2,128]{2,1,0:T(2,128)(2,1)} %taps_ref.3), custom_call_target="tpu_custom_call" | custom-call | tf_op jit(solution)/shard_map/compress/pallas_call | solution.py:67
  4.5 4.7 %all-to-all-start.1 = ((bf16[8,2,8,3,16,128]{5,4,3,2,1,0:T(8,128)(2,1)}), bf16[8,2,8,3,16,128]{5,4,3,2,1,0:T(8,128)(2,1)S(1)}, u32[]{:S(2)}, u32[]{:S(2)}) async-start(bf16[8,2,8,3,16,128]{5,4,3,2,1,0:T(8,128)(2,1)} %compress.1), calls=%async_computation.1 | async-start | bytes 3145728 | tf_op jit(solution)/shard_map/all_to_all | solution.py:253
  9.2 6.7 %compress_relative.1 = (bf16[4,2,8,5,16,128]{5,4,3,2,1,0:T(8,128)(2,1)}, bf16[4,2,8,5,16,128]{5,4,3,2,1,0:T(8,128)(2,1)}) custom-call(s32[1]{0:T(128)} %bitcast.1.band_ref, bf16[16,8,128,128]{3,2,1,0:T(8,128)(2,1)} %bitcast.35, bf16[8,2,128]{2,1,0:T(2,128)(2,1)} %taps_ref.3), custom_call_target="tpu_custom_call" | custom-call | tf_op jit(solution)/shard_map/compress_relative/pallas_call | solution.py:67
  15.8 0.5 collective-permute-start
  16.4 0.1 mul.15
  16.4 0.1 reshape.113
  16.5 0.4 convert_reduce_fusion
  17.0 0.1 select_reduce_fusion
  17.1 0.1 copy.18
  17.2 0.7 sub.7.ids_ref
  17.9 0.2 fusion
  18.2 0.7 compare_reduce_fusion
  18.9 0.7 pad_maximum_fusion.3
  19.6 1.5 fusion.5
  21.1 0.0 collective-permute-done
  21.1 1.5 fusion.6
  22.6 0.9 pad_maximum_fusion.2
  23.5 1.2 pad_maximum_fusion
  24.8 6.0 %all-to-all-done.1 = bf16[8,2,8,3,16,128]{5,4,3,2,1,0:T(8,128)(2,1)S(1)} async-done(((bf16[8,2,8,3,16,128]{5,4,3,2,1,0:T(8,128)(2,1)}), bf16[8,2,8,3,16,128]{5,4,3,2,1,0:T(8,128)(2,1)S(1)}, u32[]{:S(2)}, u32[]{:S(2)}) %all-to-all-start.1) | async-done | bytes 1572896 | tf_op jit(solution)/shard_map/all_to_all | solution.py:253
  30.7 0.6 collective-permute-start.1
  31.3 2.1 %collective-permute-start.2 = (bf16[2,2,8,5,16,128]{5,4,3,2,1,0:T(8,128)(2,1)}, bf16[2,2,8,5,16,128]{5,4,3,2,1,0:T(8,128)(2,1)}, u32[]{:S(2)}, u32[]{:S(2)}) collective-permute-start(bf16[2,2,8,5,16,128]{5,4,3,2,1,0:T(8,128)(2,1)} %get-tuple-element.41), channel_id=1, source_target_pairs={{0,4},{1,5},{2,6},{3,7},{4,0},{5,1},{6,2},{7,3},{8,12},{9,13},{10,... | collective-permute-start | bytes 1966088 | tf_op jit(solution)/shard_map/ppermute | solution.py:262
  33.4 0.6 collective-permute-start.3
  34.7 48.6 %conditional.1 = (bf16[32,8,48,128]{3,2,1,0:T(8,128)(2,1)}) conditional(s32[]{:T(128)} %convert_element_type.9, () %tuple.14, (bf16[8,2,8,3,16,128]{5,4,3,2,1,0:T(8,128)(2,1)S(1)}, s32[16]{0:T(128)S(1)}, s32[1]{0:T(128)}) %tuple.15), branch_computations={%region_3.4_spmd, %region_4.5_spmd} | conditional | bytes 6291464 | solution.py:234
  34.7 1.8 %pack.2 = bf16[32,8,48,128]{3,2,1,0:T(8,128)(2,1)} custom-call(s32[16]{0:T(128)S(1)} %get-tuple-element.15.table_ref, s32[1]{0:T(128)} %get-tuple-element.16.band_ref, bf16[8,2,8,48,128]{4,3,2,1,0:T(8,128)(2,1)S(1)} %bitcast.30), custom_call_target="tpu_custom_call" | custom-call | tf_op jit(solution)/shard_map/cond/branch_1_fun/pack/pallas_call | solution.py:119
  36.5 46.8 %all_to_all.14 = bf16[32,8,48,128]{3,2,1,0:T(8,128)(2,1)} all-to-all(bf16[32,8,48,128]{3,2,1,0:T(8,128)(2,1)} %pack.2), channel_id=1, replica_groups=mesh['ping'=16,'band'=8] {'ping'}, dimensions={0} | all-to-all | bytes 6291456 | tf_op jit(solution)/shard_map/cond/branch_1_fun/all_to_all | solution.py:229
  83.3 0.0 collective-permute-done.1
  83.3 0.0 collective-permute-done.2
  83.3 0.0 collective-permute-done.3
  83.3 3.4 %pack.3 = bf16[32,8,80,128]{3,2,1,0:T(8,128)(2,1)} custom-call(s32[16]{0:T(128)S(1)} %fusion.4.table_ref, s32[1]{0:T(128)} %bitcast.1.band_ref, bf16[1,2,8,80,128]{4,3,2,1,0:T(8,128)(2,1)S(1)} %bitcast.31, bf16[1,2,8,80,128]{4,3,2,1,0:T(8,128)(2,1)S(1)} %bitcast.32, bf16[2,2,8,80,128]{4,3,2,1,0:T(8,128)(2,1)S(1)} %bitcast.33, ...), custom_call_target="tpu_custom_call" | custom-call | tf_op jit(solution)/shard_map/pack/pallas_call | solution.py:119
  86.8 64.5 %all_to_all.15.refs_1_ = bf16[32,8,80,128]{3,2,1,0:T(8,128)(2,1)} all-to-all(bf16[32,8,80,128]{3,2,1,0:T(8,128)(2,1)} %pack.3), channel_id=1, replica_groups=mesh['ping'=16,'band'=8] {'ping'}, dimensions={0} | all-to-all | bytes 10485760 | tf_op jit(solution)/shard_map/all_to_all | solution.py:266
  151.2 11.9 %form_images.1 = bf16[2048,1024]{1,0:T(8,128)(2,1)} custom-call(s32[32]{0:T(128)} %sub.7.ids_ref, s32[8]{0:T(128)} %offsets_ref.1, bf16[32,8,48,128]{3,2,1,0:T(8,128)(2,1)S(1)} %copy-done.1, bf16[32,8,80,128]{3,2,1,0:T(8,128)(2,1)} %all_to_all.15.refs_1_, bf16[256,256]{1,0:T(8,128)(2,1)} %bitcast.36, bf16[8,384,128]{2,1,0:T(8,128)(2,1)} %refs_3_.1), custom_call_target="tpu_custom_call" | custom-call | tf_op jit(solution)/shard_map/form_images/pallas_call | solution.py:178
  (21 shorter events, 0.1 us)
Async XLA Ops:
  0.0 17.9 %copy-start = (bf16[2,128,64]{1,2,0:T(8,128)(2,1)S(1)}, bf16[2,128,64]{1,2,0:T(8,128)(2,1)}, u32[]{:S(2)}) copy-start(bf16[2,128,64]{1,2,0:T(8,128)(2,1)} %param.13) | copy-start | bytes 98308
  4.5 11.9 %copy-start.4 = (s32[256]{0:T(256)S(1)}, s32[256]{0:T(256)}, u32[]{:S(2)}) copy-start(s32[256]{0:T(256)} %param.17) | copy-start | bytes 3076
  4.5 12.0 %copy-start.3 = (s32[256]{0:T(256)S(1)}, s32[256]{0:T(256)}, u32[]{:S(2)}) copy-start(s32[256]{0:T(256)} %param.16) | copy-start | bytes 3076
  4.5 13.4 %copy-start.2 = (bf16[2,64,64]{2,1,0:T(8,128)(2,1)S(1)}, bf16[2,64,64]{2,1,0:T(8,128)(2,1)}, u32[]{:S(2)}) copy-start(bf16[2,64,64]{2,1,0:T(8,128)(2,1)} %param.12) | copy-start | bytes 49156
  4.5 26.3 %all-to-all-start.1 = ((bf16[8,2,8,3,16,128]{5,4,3,2,1,0:T(8,128)(2,1)}), bf16[8,2,8,3,16,128]{5,4,3,2,1,0:T(8,128)(2,1)S(1)}, u32[]{:S(2)}, u32[]{:S(2)}) async-start(bf16[8,2,8,3,16,128]{5,4,3,2,1,0:T(8,128)(2,1)} %compress.1), calls=%async_computation.1 | async-start | bytes 3145728 | tf_op jit(solution)/shard_map/all_to_all | solution.py:253
  15.8 5.3 %collective-permute-start = (bf16[4,2,8,5,16,128]{5,4,3,2,1,0:T(8,128)(2,1)}, bf16[4,2,8,5,16,128]{5,4,3,2,1,0:T(8,128)(2,1)}, u32[]{:S(2)}, u32[]{:S(2)}) collective-permute-start(bf16[4,2,8,5,16,128]{5,4,3,2,1,0:T(8,128)(2,1)} %get-tuple-element.35), channel_id=1, source_target_pairs={{0,1},{1,0},{2,3},{3,2},{4,5},{5,4},{6,7},{7,6},{8,9},{9,8},{10,11... | collective-permute-start | bytes 3932168 | tf_op jit(solution)/shard_map/ppermute | solution.py:255
  30.7 52.5 %collective-permute-start.1 = (bf16[2,2,8,5,16,128]{5,4,3,2,1,0:T(8,128)(2,1)}, bf16[2,2,8,5,16,128]{5,4,3,2,1,0:T(8,128)(2,1)S(1)}, u32[]{:S(2)}, u32[]{:S(2)}) collective-permute-start(bf16[2,2,8,5,16,128]{5,4,3,2,1,0:T(8,128)(2,1)} %get-tuple-element.40), channel_id=1, source_target_pairs={{0,2},{1,3},{2,4},{3,5},{4,6},{5,7},{6,0},{7,1},{8,10},{9,11},{10,... | collective-permute-start | bytes 1966088 | tf_op jit(solution)/shard_map/ppermute | solution.py:262
  31.3 52.0 %collective-permute-start.2 = (bf16[2,2,8,5,16,128]{5,4,3,2,1,0:T(8,128)(2,1)}, bf16[2,2,8,5,16,128]{5,4,3,2,1,0:T(8,128)(2,1)}, u32[]{:S(2)}, u32[]{:S(2)}) collective-permute-start(bf16[2,2,8,5,16,128]{5,4,3,2,1,0:T(8,128)(2,1)} %get-tuple-element.41), channel_id=1, source_target_pairs={{0,4},{1,5},{2,6},{3,7},{4,0},{5,1},{6,2},{7,3},{8,12},{9,13},{10,... | collective-permute-start | bytes 1966088 | tf_op jit(solution)/shard_map/ppermute | solution.py:262
  33.4 49.9 %collective-permute-start.3 = (bf16[2,2,8,5,16,128]{5,4,3,2,1,0:T(8,128)(2,1)}, bf16[2,2,8,5,16,128]{5,4,3,2,1,0:T(8,128)(2,1)}, u32[]{:S(2)}, u32[]{:S(2)}) collective-permute-start(bf16[2,2,8,5,16,128]{5,4,3,2,1,0:T(8,128)(2,1)} %pad_maximum_fusion.2), channel_id=1, source_target_pairs={{0,6},{1,7},{2,0},{3,1},{4,2},{5,3},{6,4},{7,5},{8,14},{9,15},{10,... | collective-permute-start | bytes 1966088 | tf_op jit(solution)/shard_map/ppermute | solution.py:262
  86.7 64.5 %copy-start.1 = (bf16[32,8,48,128]{3,2,1,0:T(8,128)(2,1)S(1)}, bf16[32,8,48,128]{3,2,1,0:T(8,128)(2,1)}, u32[]{:S(2)}) copy-start(bf16[32,8,48,128]{3,2,1,0:T(8,128)(2,1)} %get-tuple-element.64.refs_0_) | copy-start | bytes 9437188

commit v10 on v9

--- a/solution.py
+++ b/solution.py
@@ -256,8 +256,8 @@
     ring = [jnp.stack([same[step], other[step]]) for step in (1, 2, 3)]
     same, other = same[:1], other[:1]
     some = jnp.any(merge_owner >= 0)
-    band_tile, table, ids, angle, some, same, other, *ring = lax.optimization_barrier(
-        (band_tile, table, ids, angle, some, same, other, *ring)
+    band_tile, table, ids, angle, some, same, other = lax.optimization_barrier(
+        (band_tile, table, ids, angle, some, same, other)
     )
     ring = [lax.ppermute(part, "band", ring_step(step + 1, 0)) for step, part in enumerate(ring)]
     first = to_owners(some, table, band, flat(band_tile))

time: 164 us -> 163 us (level)
  waiting for transfers between devices: 5.99 us -> 0.01 us
  starting transfers between devices: 8.44 us -> 11 us
    all_to_all x1, waiting for transfers between devices: 5.98 us -> 0.01 us  [on_device(): lax.all_to_all(sent, 'band', split_axis=0, concat_axis=0, tiled=True)]
    ppermute x3, starting transfers between devices: 3.24 us -> 5.82 us  [on_device(): lax.ppermute(part, 'band', ring_step(step + 1, 0))]
  transfers between devices with their start and end apart: 5 -> 5, of which waited for: 1 -> 0; matrix products, arithmetic and copies ran while one was open for 5% -> 6% of each run, Pallas kernels for 5% -> 5%
where the time goes in v10:
time: 163 us; the launch traced here: 162 us
  blocking collectives  112 us (69%)
  Pallas kernels  28.2 us (17%)
  starting transfers between devices  11 us (7%)
  other arithmetic  4.78 us (3%)
  local copies, waits for them, and re-layouts  4.75 us (3%)
    all_to_all x1, blocking collectives, on_device(): lax.all_to_all(outgoing, 'ping', split_axis=0, concat_axis=0, tiled=True)  64.9 us
    all_to_all x1, blocking collectives, exchange(): lax.all_to_all(pack(table, band, source), 'ping', split_axis=0, concat_ax...  47.2 us
    pallas_call x1, Pallas kernels, form_images(): pl.pallas_call(functools.partial(image_kernel, chunks), grid_spec=pltpu.P...  11.9 us
    pallas_call x2, Pallas kernels, compress(): pl.pallas_call(functools.partial(compress_kernel, relative), grid_spec=pl...  11.1 us
    ppermute x3, starting transfers between devices, on_device(): lax.ppermute(part, 'band', ring_step(step + 1, 0))  5.82 us
    pallas_call x2, Pallas kernels, pack(): pl.pallas_call(functools.partial(pack_kernel, len(sources) > 1), grid_spe...  5.14 us
    all_to_all x1, starting transfers between devices, on_device(): lax.all_to_all(sent, 'band', split_axis=0, concat_axis=0, tiled=True)  4.7 us
    slice x2, local copies, waits for them, and re-layouts, on_device(): ring = [jnp.stack([same[step], other[step]]) for step in (1, 2, 3)]  3.77 us
  transfers between devices with their start and end apart: 5, of which 0 were waited for; matrix products, arithmetic and copies ran while one was open for 6% of the time, Pallas kernels for 5%

profile of v10, /device:TPU:0, one launch (start us, length us, event | category | flops | bytes accessed | tf_op | source)
XLA Modules:
  0.0 161.9 jit_solution(17494134573661919855)
XLA Ops:
  0.0 4.4 %compress.1 = bf16[8,2,8,3,16,128]{5,4,3,2,1,0:T(8,128)(2,1)} custom-call(s32[1]{0:T(128)} %bitcast.1.band_ref, bf16[16,8,128,128]{3,2,1,0:T(8,128)(2,1)} %bitcast.34, bf16[8,2,128]{2,1,0:T(2,128)(2,1)} %taps_ref.3), custom_call_target="tpu_custom_call" | custom-call | tf_op jit(solution)/shard_map/compress/pallas_call | solution.py:67
  4.5 4.7 %all-to-all-start.1 = ((bf16[8,2,8,3,16,128]{5,4,3,2,1,0:T(8,128)(2,1)}), bf16[8,2,8,3,16,128]{5,4,3,2,1,0:T(8,128)(2,1)S(1)}, u32[]{:S(2)}, u32[]{:S(2)}) async-start(bf16[8,2,8,3,16,128]{5,4,3,2,1,0:T(8,128)(2,1)} %compress.1), calls=%async_computation.1 | async-start | bytes 3145728 | tf_op jit(solution)/shard_map/all_to_all | solution.py:253
  9.2 6.7 %compress_relative.1 = (bf16[4,2,8,5,16,128]{5,4,3,2,1,0:T(8,128)(2,1)}, bf16[4,2,8,5,16,128]{5,4,3,2,1,0:T(8,128)(2,1)}) custom-call(s32[1]{0:T(128)} %bitcast.1.band_ref, bf16[16,8,128,128]{3,2,1,0:T(8,128)(2,1)} %bitcast.35, bf16[8,2,128]{2,1,0:T(2,128)(2,1)} %taps_ref.3), custom_call_target="tpu_custom_call" | custom-call | tf_op jit(solution)/shard_map/compress_relative/pallas_call | solution.py:67
  15.8 0.5 collective-permute-start
  16.4 0.1 reshape.113
  16.4 0.4 convert_reduce_fusion
  16.9 0.1 mul.15
  17.0 0.1 select_reduce_fusion
  17.1 0.2 fusion
  17.3 2.2 %fusion.5 = (bf16[1,2,8,5,16,128]{5,4,3,2,1,0:T(8,128)(2,1)S(1)}, bf16[1,2,8,5,16,128]{5,4,3,2,1,0:T(8,128)(2,1)}, bf16[1,2,8,5,16,128]{5,4,3,2,1,0:T(8,128)(2,1)S(1)}, bf16[1,2,8,5,16,128]{5,4,3,2,1,0:T(8,128)(2,1)S(1)}) fusion(bf16[4,2,8,5,16,128]{5,4,3,2,1,0:T(8,128)(2,1)} %get-tuple-element.31), kind=kLoop, calls=%fused_computation.26 | loop fusion | bytes 2621440 | tf_op jit(solution)/shard_map/slice | solution.py:256
  19.6 0.1 copy.18
  19.6 0.7 sub.7.ids_ref
  20.3 0.0 collective-permute-done
  20.3 1.6 fusion.6
  21.9 0.9 pad_maximum_fusion
  22.8 1.7 %collective-permute-start.1 = (bf16[2,2,8,5,16,128]{5,4,3,2,1,0:T(8,128)(2,1)}, bf16[2,2,8,5,16,128]{5,4,3,2,1,0:T(8,128)(2,1)S(1)}, u32[]{:S(2)}, u32[]{:S(2)}) collective-permute-start(bf16[2,2,8,5,16,128]{5,4,3,2,1,0:T(8,128)(2,1)} %pad_maximum_fusion), channel_id=1, source_target_pairs={{0,2},{1,3},{2,4},{3,5},{4,6},{5,7},{6,0},{7,1},{8,10},{9,11},{10,... | collective-permute-start | bytes 1966088 | tf_op jit(solution)/shard_map/ppermute | solution.py:262
  24.5 0.9 pad_maximum_fusion.1
  25.4 2.7 %collective-permute-start.2 = (bf16[2,2,8,5,16,128]{5,4,3,2,1,0:T(8,128)(2,1)}, bf16[2,2,8,5,16,128]{5,4,3,2,1,0:T(8,128)(2,1)}, u32[]{:S(2)}, u32[]{:S(2)}) collective-permute-start(bf16[2,2,8,5,16,128]{5,4,3,2,1,0:T(8,128)(2,1)} %pad_maximum_fusion.1), channel_id=1, source_target_pairs={{0,4},{1,5},{2,6},{3,7},{4,0},{5,1},{6,2},{7,3},{8,12},{9,13},{10,... | collective-permute-start | bytes 1966088 | tf_op jit(solution)/shard_map/ppermute | solution.py:262
  28.1 1.0 pad_maximum_fusion.2
  29.0 1.5 collective-permute-start.3
  30.6 0.7 compare_reduce_fusion
  31.3 0.7 pad_maximum_fusion.3
  32.0 0.0 all-to-all-done.1
  32.6 49.0 %conditional.1 = (bf16[32,8,48,128]{3,2,1,0:T(8,128)(2,1)}) conditional(s32[]{:T(128)} %convert_element_type.9, () %tuple.14, (bf16[8,2,8,3,16,128]{5,4,3,2,1,0:T(8,128)(2,1)S(1)}, s32[16]{0:T(128)S(1)}, s32[1]{0:T(128)}) %tuple.15), branch_computations={%region_3.4_spmd, %region_4.5_spmd} | conditional | bytes 6291464 | solution.py:234
  32.6 1.7 %pack.2 = bf16[32,8,48,128]{3,2,1,0:T(8,128)(2,1)} custom-call(s32[16]{0:T(128)S(1)} %get-tuple-element.15.table_ref, s32[1]{0:T(128)} %get-tuple-element.16.band_ref, bf16[8,2,8,48,128]{4,3,2,1,0:T(8,128)(2,1)S(1)} %bitcast.30), custom_call_target="tpu_custom_call" | custom-call | tf_op jit(solution)/shard_map/cond/branch_1_fun/pack/pallas_call | solution.py:119
  34.4 47.2 %all_to_all.14 = bf16[32,8,48,128]{3,2,1,0:T(8,128)(2,1)} all-to-all(bf16[32,8,48,128]{3,2,1,0:T(8,128)(2,1)} %pack.2), channel_id=1, replica_groups=mesh['ping'=16,'band'=8] {'ping'}, dimensions={0} | all-to-all | bytes 6291456 | tf_op jit(solution)/shard_map/cond/branch_1_fun/all_to_all | solution.py:229
  81.6 0.0 collective-permute-done.1
  81.6 0.0 collective-permute-done.2
  81.6 0.0 collective-permute-done.3
  81.6 3.4 %pack.3 = bf16[32,8,80,128]{3,2,1,0:T(8,128)(2,1)} custom-call(s32[16]{0:T(128)S(1)} %fusion.4.table_ref, s32[1]{0:T(128)} %bitcast.1.band_ref, bf16[1,2,8,80,128]{4,3,2,1,0:T(8,128)(2,1)S(1)} %bitcast.31, bf16[1,2,8,80,128]{4,3,2,1,0:T(8,128)(2,1)S(1)} %bitcast.32, bf16[2,2,8,80,128]{4,3,2,1,0:T(8,128)(2,1)S(1)} %bitcast.33, ...), custom_call_target="tpu_custom_call" | custom-call | tf_op jit(solution)/shard_map/pack/pallas_call | solution.py:119
  85.0 64.9 %all_to_all.15.refs_1_ = bf16[32,8,80,128]{3,2,1,0:T(8,128)(2,1)} all-to-all(bf16[32,8,80,128]{3,2,1,0:T(8,128)(2,1)} %pack.3), channel_id=1, replica_groups=mesh['ping'=16,'band'=8] {'ping'}, dimensions={0} | all-to-all | bytes 10485760 | tf_op jit(solution)/shard_map/all_to_all | solution.py:266
  150.0 11.9 %form_images.1 = bf16[2048,1024]{1,0:T(8,128)(2,1)} custom-call(s32[32]{0:T(128)} %sub.7.ids_ref, s32[8]{0:T(128)} %offsets_ref.1, bf16[32,8,48,128]{3,2,1,0:T(8,128)(2,1)S(1)} %copy-done.1, bf16[32,8,80,128]{3,2,1,0:T(8,128)(2,1)} %all_to_all.15.refs_1_, bf16[256,256]{1,0:T(8,128)(2,1)} %bitcast.36, bf16[8,384,128]{2,1,0:T(8,128)(2,1)} %refs_3_.1), custom_call_target="tpu_custom_call" | custom-call | tf_op jit(solution)/shard_map/form_images/pallas_call | solution.py:178
  (24 shorter events, 0.1 us)
Async XLA Ops:
  0.0 17.1 %copy-start = (bf16[2,128,64]{1,2,0:T(8,128)(2,1)S(1)}, bf16[2,128,64]{1,2,0:T(8,128)(2,1)}, u32[]{:S(2)}) copy-start(bf16[2,128,64]{1,2,0:T(8,128)(2,1)} %param.13) | copy-start | bytes 98308
  4.5 11.9 %copy-start.5 = (s32[256]{0:T(256)S(1)}, s32[256]{0:T(256)}, u32[]{:S(2)}) copy-start(s32[256]{0:T(256)} %param.17) | copy-start | bytes 3076
  4.5 11.9 %copy-start.4 = (s32[256]{0:T(256)S(1)}, s32[256]{0:T(256)}, u32[]{:S(2)}) copy-start(s32[256]{0:T(256)} %param.16) | copy-start | bytes 3076
  4.5 12.6 %copy-start.3 = (bf16[2,64,64]{2,1,0:T(8,128)(2,1)S(1)}, bf16[2,64,64]{2,1,0:T(8,128)(2,1)}, u32[]{:S(2)}) copy-start(bf16[2,64,64]{2,1,0:T(8,128)(2,1)} %param.12) | copy-start | bytes 49156
  4.5 27.5 %all-to-all-start.1 = ((bf16[8,2,8,3,16,128]{5,4,3,2,1,0:T(8,128)(2,1)}), bf16[8,2,8,3,16,128]{5,4,3,2,1,0:T(8,128)(2,1)S(1)}, u32[]{:S(2)}, u32[]{:S(2)}) async-start(bf16[8,2,8,3,16,128]{5,4,3,2,1,0:T(8,128)(2,1)} %compress.1), calls=%async_computation.1 | async-start | bytes 3145728 | tf_op jit(solution)/shard_map/all_to_all | solution.py:253
  15.8 4.5 %collective-permute-start = (bf16[4,2,8,5,16,128]{5,4,3,2,1,0:T(8,128)(2,1)}, bf16[4,2,8,5,16,128]{5,4,3,2,1,0:T(8,128)(2,1)}, u32[]{:S(2)}, u32[]{:S(2)}) collective-permute-start(bf16[4,2,8,5,16,128]{5,4,3,2,1,0:T(8,128)(2,1)} %get-tuple-element.32), channel_id=1, source_target_pairs={{0,1},{1,0},{2,3},{3,2},{4,5},{5,4},{6,7},{7,6},{8,9},{9,8},{10,11... | collective-permute-start | bytes 3932168 | tf_op jit(solution)/shard_map/ppermute | solution.py:255
  20.3 4.2 %copy-start.2 = (bf16[1,2,8,5,16,128]{5,4,3,2,1,0:T(8,128)(2,1)S(1)}, bf16[1,2,8,5,16,128]{5,4,3,2,1,0:T(8,128)(2,1)}, u32[]{:S(2)}) copy-start(bf16[1,2,8,5,16,128]{5,4,3,2,1,0:T(8,128)(2,1)} %get-tuple-element.45) | copy-start | bytes 983044
  22.8 58.8 %collective-permute-start.1 = (bf16[2,2,8,5,16,128]{5,4,3,2,1,0:T(8,128)(2,1)}, bf16[2,2,8,5,16,128]{5,4,3,2,1,0:T(8,128)(2,1)S(1)}, u32[]{:S(2)}, u32[]{:S(2)}) collective-permute-start(bf16[2,2,8,5,16,128]{5,4,3,2,1,0:T(8,128)(2,1)} %pad_maximum_fusion), channel_id=1, source_target_pairs={{0,2},{1,3},{2,4},{3,5},{4,6},{5,7},{6,0},{7,1},{8,10},{9,11},{10,... | collective-permute-start | bytes 1966088 | tf_op jit(solution)/shard_map/ppermute | solution.py:262
  25.4 56.2 %collective-permute-start.2 = (bf16[2,2,8,5,16,128]{5,4,3,2,1,0:T(8,128)(2,1)}, bf16[2,2,8,5,16,128]{5,4,3,2,1,0:T(8,128)(2,1)}, u32[]{:S(2)}, u32[]{:S(2)}) collective-permute-start(bf16[2,2,8,5,16,128]{5,4,3,2,1,0:T(8,128)(2,1)} %pad_maximum_fusion.1), channel_id=1, source_target_pairs={{0,4},{1,5},{2,6},{3,7},{4,0},{5,1},{6,2},{7,3},{8,12},{9,13},{10,... | collective-permute-start | bytes 1966088 | tf_op jit(solution)/shard_map/ppermute | solution.py:262
  29.0 52.6 %collective-permute-start.3 = (bf16[2,2,8,5,16,128]{5,4,3,2,1,0:T(8,128)(2,1)}, bf16[2,2,8,5,16,128]{5,4,3,2,1,0:T(8,128)(2,1)}, u32[]{:S(2)}, u32[]{:S(2)}) collective-permute-start(bf16[2,2,8,5,16,128]{5,4,3,2,1,0:T(8,128)(2,1)} %pad_maximum_fusion.2), channel_id=1, source_target_pairs={{0,6},{1,7},{2,0},{3,1},{4,2},{5,3},{6,4},{7,5},{8,14},{9,15},{10,... | collective-permute-start | bytes 1966088 | tf_op jit(solution)/shard_map/ppermute | solution.py:262
  85.0 64.9 %copy-start.1 = (bf16[32,8,48,128]{3,2,1,0:T(8,128)(2,1)S(1)}, bf16[32,8,48,128]{3,2,1,0:T(8,128)(2,1)}, u32[]{:S(2)}) copy-start(bf16[32,8,48,128]{3,2,1,0:T(8,128)(2,1)} %get-tuple-element.56.refs_0_) | copy-start | bytes 9437188
